TPU v7x, 512 devices: a whole 4x4x16 slice. The times are simulated.
512 devices in a mesh: tm: 256 (over y, x, z_lo, core), chan: 2 (over z_hi).
Axes of the slice: x: 4, y: 4, z: 16 (z_hi: 2, z_lo: 8; z = z_hi * 8 + z_lo), core: 2. Of those that a mesh axis runs over, the one named last changes fastest.
Arguments:
- signal: bfloat16 [131072, 256], P('tm', 'chan'), may hold values from -6 to 6
- skip_in: bfloat16 [131072, 256], P('tm', 'chan'), may hold values from -6 to 6
- tap_weight: bfloat16 [4, 2, 256, 512], replicated, may hold values from -0.25 to 0.25
- tap_bias: float32 [4, 512], replicated, may hold values from -3 to 3
- res_weight: bfloat16 [3, 256, 256], replicated, may hold values from -0.375 to 0.375
- skip_weight: bfloat16 [4, 256, 256], replicated, may hold values from -0.375 to 0.375
- head_w1: float32 [256, 256], replicated, may hold values from -0.375 to 0.375
- head_b1: float32 [256], replicated, may hold values from -3 to 3
- head_w2: float32 [256, 12], replicated, may hold values from -0.375 to 0.375
- head_second_bias: float32 [12], replicated, may hold values from -3 to 3
- event_bin: int32 [1024], P('tm'), may hold values from 0 to 15
- observed: int32 [1024], P('tm'), may hold values 0 or 1
- valid_len: int32 [1], replicated, may hold values from 130817 to 131072
Outputs:
- window_nll: float32 [1024], P(('tm', 'chan'))
- grad_input: bfloat16 [131072, 256], P('tm', 'chan')
All inputs are finite; a program needn't handle non-finite values. No bound on the sum of `observed` on one device may be relied on, other than what follows from the above.
Results may differ from a plain program's by a relative error of at most 0.022.
Values may be sent and summed in bfloat16 or wider, within the bound.
No kernel may reach another device: no remote copies, remote signals or barrier semaphores. Data moves between devices by JAX's collectives and lax.ppermute only.
A program may use at most 64 MiB of HBM per device.

v0:
```python
import jax
import jax.numpy as jnp
from jax import lax
from jax.sharding import PartitionSpec as P

WLEN = 128


def passed_along(block, axis, distance):
    devices = range(lax.axis_size(axis))
    route = [(i - distance, i) for i in devices if i - distance in devices]
    return lax.ppermute(block, axis, route)


def gate_values(preact, half_width):
    filters = jnp.tanh(preact[:, :half_width])
    gates = jax.nn.sigmoid(preact[:, half_width:])
    return (filters * gates).astype(jnp.bfloat16)


def gate_grads(preact, grad_gated, half_width):
    filters = jnp.tanh(preact[:, :half_width])
    gates = jax.nn.sigmoid(preact[:, half_width:])
    grad_filter = grad_gated * gates * (1.0 - filters * filters)
    gate_gradient = grad_gated * filters * gates * (1.0 - gates)
    return jnp.concatenate([grad_filter, gate_gradient], axis=1).astype(jnp.bfloat16)


def silu_slope(values):
    sig = jax.nn.sigmoid(values)
    return sig * (1.0 + values * (1.0 - sig))


def pool_windows(activity, keep_mask, window_len):
    row_count, width = activity.shape
    sums = (
        (activity * keep_mask[:, None])
        .reshape(row_count // window_len, window_len, width)
        .sum(axis=1)
    )
    counts = keep_mask.reshape(row_count // window_len, window_len).sum(axis=1)
    return sums / jnp.maximum(counts, 1.0)[:, None]


def window_loss(pooled, bins, flags, head_w1, head_b1, head_w2, head_second_bias):
    hidden = jax.nn.silu(jnp.dot(pooled, head_w1, precision=lax.Precision.HIGHEST) + head_b1)
    params = jnp.dot(hidden, head_w2, precision=lax.Precision.HIGHEST) + head_second_bias
    mixes = params.shape[1] // 3
    logits = 4.0 * jnp.tanh(params[:, :mixes])
    mixture_log_weight = logits - jnp.log(jnp.sum(jnp.exp(logits), axis=1, keepdims=True))
    log_scale = jnp.tanh(params[:, mixes : 2 * mixes])
    log_shape = 0.5 * jnp.tanh(params[:, 2 * mixes :])
    shape_value = jnp.exp(log_shape)
    log_time = jnp.log((bins.astype(jnp.float32) + 1.0) / 8.0)[:, None]
    ratio = log_time - log_scale
    power = jnp.exp(shape_value * ratio)
    log_density = log_shape - log_scale + (shape_value - 1.0) * ratio - power
    component = jnp.where(flags[:, None] == 1, log_density, -power)
    return -jnp.log(jnp.sum(jnp.exp(mixture_log_weight + component), axis=1))


def head_grads(pooled, bins, flags, head_w1, head_b1, head_w2, head_second_bias):

    def loss_of(values):
        return window_loss(values, bins, flags, head_w1, head_b1, head_w2, head_second_bias)

    nll_values, pullback = jax.vjp(loss_of, pooled)
    return (nll_values, pullback(jnp.ones_like(nll_values))[0])


def spread_rows(grad_pool, window_len):
    window_total_count, width = grad_pool.shape
    return jnp.broadcast_to(grad_pool[:, None, :], (window_total_count, window_len, width)).reshape(
        window_total_count * window_len, width
    )


def delay(values, shard_shift):
    return passed_along(values, "tm", shard_shift)


def advance(values, shard_shift):
    return passed_along(values, "tm", -shard_shift)


def own_columns(matrix, chan_at, chan_part, width):
    filter_cols = lax.dynamic_slice_in_dim(matrix, chan_at * chan_part, chan_part, 1)
    gate_cols = lax.dynamic_slice_in_dim(matrix, width + chan_at * chan_part, chan_part, 1)
    return jnp.concatenate([filter_cols, gate_cols], axis=1)


def local(
    signal,
    skip_in,
    tap_weight,
    tap_bias,
    res_weight,
    skip_weight,
    head_w1,
    head_b1,
    head_w2,
    head_second_bias,
    event_bin,
    observed,
    valid_len,
):
    chan_count = lax.axis_size("chan")
    chan_at = lax.axis_index("chan")
    shard_at = lax.axis_index("tm")
    shard_rows, chan_part = signal.shape
    width = chan_part * chan_count
    layers = tap_weight.shape[0]
    base_shift = lax.axis_size("tm") // 16
    windows_here = shard_rows // WLEN
    own_windows = windows_here // chan_count
    limit = valid_len[0]
    current = signal
    skip_sum = skip_in.astype(jnp.float32)
    preacts = []
    for layer_number in range(layers):
        tap_old = own_columns(tap_weight[layer_number, 0], chan_at, chan_part, width)
        tap_new = own_columns(tap_weight[layer_number, 1], chan_at, chan_part, width)
        bias_own = own_columns(tap_bias[layer_number][None, :], chan_at, chan_part, width)[0]
        whole = lax.all_gather(current, "chan", axis=1, tiled=True)
        delayed = delay(whole, base_shift * 2**layer_number)
        preact = jnp.dot(delayed, tap_old, preferred_element_type=jnp.float32)
        preact = preact + jnp.dot(whole, tap_new, preferred_element_type=jnp.float32) + bias_own
        gated = gate_values(preact, chan_part)
        preacts.append(preact)
        gated_all = lax.all_gather(gated, "chan", axis=1, tiled=True)
        if layer_number < layers - 1:
            res_cols = lax.dynamic_slice_in_dim(
                res_weight[layer_number], chan_at * chan_part, chan_part, 1
            )
            current = (
                current.astype(jnp.float32)
                + jnp.dot(gated_all, res_cols, preferred_element_type=jnp.float32)
            ).astype(jnp.bfloat16)
        skip_cols = lax.dynamic_slice_in_dim(
            skip_weight[layer_number], chan_at * chan_part, chan_part, 1
        )
        skip_sum = skip_sum + jnp.dot(gated_all, skip_cols, preferred_element_type=jnp.float32)
    positions = shard_at * shard_rows + jnp.arange(shard_rows, dtype=jnp.int32)
    keep_mask = (positions < limit).astype(jnp.float32)
    pooled_part = pool_windows(jax.nn.silu(skip_sum), keep_mask, WLEN)
    pooled = lax.all_gather(pooled_part, "chan", axis=1, tiled=True)
    nll_all, grad_pool = head_grads(
        pooled, event_bin, observed, head_w1, head_b1, head_w2, head_second_bias
    )
    nll_values = lax.dynamic_slice_in_dim(nll_all, chan_at * own_windows, own_windows, 0)
    pool_part = lax.dynamic_slice_in_dim(grad_pool, chan_at * chan_part, chan_part, 1)
    grad_skip = (spread_rows(pool_part, WLEN) * keep_mask[:, None] * silu_slope(skip_sum)).astype(
        jnp.bfloat16
    )
    skip_grads_all = lax.all_gather(grad_skip, "chan", axis=1, tiled=True)
    grad_rows = None
    for layer_number in range(layers - 1, -1, -1):
        tap_old = own_columns(tap_weight[layer_number, 0], chan_at, chan_part, width)
        tap_new = own_columns(tap_weight[layer_number, 1], chan_at, chan_part, width)
        skip_rows = lax.dynamic_slice_in_dim(
            skip_weight[layer_number], chan_at * chan_part, chan_part, 0
        )
        grad_gated = jnp.dot(skip_grads_all, skip_rows.T, preferred_element_type=jnp.float32)
        if grad_rows is not None:
            rows_all = lax.all_gather(grad_rows, "chan", axis=1, tiled=True)
            res_rows = lax.dynamic_slice_in_dim(
                res_weight[layer_number], chan_at * chan_part, chan_part, 0
            )
            grad_gated = grad_gated + jnp.dot(
                rows_all, res_rows.T, preferred_element_type=jnp.float32
            )
        preactivation_gradient = gate_grads(preacts[layer_number], grad_gated, chan_part)
        ahead = advance(preactivation_gradient, base_shift * 2**layer_number)
        partial_sum = jnp.dot(preactivation_gradient, tap_new.T, preferred_element_type=jnp.float32)
        partial_sum = partial_sum + jnp.dot(ahead, tap_old.T, preferred_element_type=jnp.float32)
        own_sum = lax.psum_scatter(
            partial_sum.astype(jnp.bfloat16), "chan", scatter_dimension=1, tiled=True
        ).astype(jnp.float32)
        if grad_rows is not None:
            own_sum = own_sum + grad_rows.astype(jnp.float32)
        grad_rows = own_sum.astype(jnp.bfloat16)
    return (nll_values, grad_rows)


def solution(mesh):
    return jax.shard_map(
        local,
        mesh=mesh,
        in_specs=(
            P("tm", "chan"),
            P("tm", "chan"),
            P(),
            P(),
            P(),
            P(),
            P(),
            P(),
            P(),
            P(),
            P("tm"),
            P("tm"),
            P(),
        ),
        out_specs=(P(("tm", "chan")), P("tm", "chan")),
        check_vma=False,
    )
```

profile of v0, /device:TPU:1, one launch (start us, length us, event | category | flops | bytes accessed | tf_op | source)
XLA Modules:
  0.0 492.4 jit_solution(5737684357259308998)
XLA Ops:
  7.2 19.5 %all_gather.39 = bf16[512,256]{1,0:T(8,128)(2,1)S(1)} all-gather(bf16[512,128]{1,0:T(8,128)(2,1)} %param.13), channel_id=1, replica_groups=mesh['tm'=256,'chan'=2] {'chan'}, dimensions={1}, use_global_device_ids=true | all-gather | bytes 393216 | tf_op jit(solution)/shard_map/all_gather | solution.py:124
  40.8 13.2 %all_gather.40 = bf16[512,256]{0,1:T(8,128)(2,1)S(1)} all-gather(bf16[512,128]{0,1:T(8,128)(2,1)S(1)} %multiply_convert_fusion.11), channel_id=1, replica_groups=mesh['tm'=256,'chan'=2] {'chan'}, dimensions={1}, use_global_device_ids=true | all-gather | bytes 393216 | tf_op jit(solution)/shard_map/all_gather | solution.py:130
  54.2 21.1 %all_gather.41 = bf16[512,256]{1,0:T(8,128)(2,1)S(1)} all-gather(bf16[512,128]{1,0:T(8,128)(2,1)S(1)} %fusion.9), channel_id=1, replica_groups=mesh['tm'=256,'chan'=2] {'chan'}, dimensions={1}, use_global_device_ids=true | all-gather | bytes 393216 | tf_op jit(solution)/shard_map/all_gather | solution.py:124
  79.7 4.3 collective-permute-done.1
  84.5 13.2 %all_gather.42 = bf16[512,256]{0,1:T(8,128)(2,1)S(1)} all-gather(bf16[512,128]{0,1:T(8,128)(2,1)S(1)} %multiply_convert_fusion.10), channel_id=1, replica_groups=mesh['tm'=256,'chan'=2] {'chan'}, dimensions={1}, use_global_device_ids=true | all-gather | bytes 393216 | tf_op jit(solution)/shard_map/all_gather | solution.py:130
  98.0 13.9 %all_gather.43 = bf16[512,256]{1,0:T(8,128)(2,1)S(1)} all-gather(bf16[512,128]{1,0:T(8,128)(2,1)S(1)} %fusion.10), channel_id=1, replica_groups=mesh['tm'=256,'chan'=2] {'chan'}, dimensions={1}, use_global_device_ids=true | all-gather | bytes 393216 | tf_op jit(solution)/shard_map/all_gather | solution.py:124
  111.9 5.1 %collective-permute-start.2 = (bf16[512,256]{1,0:T(8,128)(2,1)S(1)}, bf16[512,256]{1,0:T(8,128)(2,1)S(1)}, u32[]{:S(2)}, u32[]{:S(2)}) collective-permute-start(bf16[512,256]{1,0:T(8,128)(2,1)S(1)} %all_gather.43), channel_id=1, source_target_pairs={{0,128},{2,130},{4,132},{6,134},{8,136},{10,138},{12,140},{14,142}... | collective-permute-start | bytes 786440 | tf_op jit(solution)/shard_map/ppermute | solution.py:12
  120.7 14.2 %all_gather.44 = bf16[512,256]{0,1:T(8,128)(2,1)S(1)} all-gather(bf16[512,128]{0,1:T(8,128)(2,1)S(1)} %multiply_convert_fusion.9), channel_id=1, replica_groups=mesh['tm'=256,'chan'=2] {'chan'}, dimensions={1}, use_global_device_ids=true | all-gather | bytes 393216 | tf_op jit(solution)/shard_map/all_gather | solution.py:130
  135.2 17.5 %all_gather.45 = bf16[512,256]{1,0:T(8,128)(2,1)S(1)} all-gather(bf16[512,128]{1,0:T(8,128)(2,1)S(1)} %fusion.11), channel_id=1, replica_groups=mesh['tm'=256,'chan'=2] {'chan'}, dimensions={1}, use_global_device_ids=true | all-gather | bytes 393216 | tf_op jit(solution)/shard_map/all_gather | solution.py:124
  152.6 5.9 %collective-permute-start.3 = (bf16[512,256]{1,0:T(8,128)(2,1)S(1)}, bf16[512,256]{1,0:T(8,128)(2,1)S(1)}, u32[]{:S(2)}, u32[]{:S(2)}) collective-permute-start(bf16[512,256]{1,0:T(8,128)(2,1)S(1)} %all_gather.45), channel_id=1, source_target_pairs={{0,256},{2,258},{4,260},{6,262},{8,264},{10,266},{12,268},{14,270}... | collective-permute-start | bytes 786440 | tf_op jit(solution)/shard_map/ppermute | solution.py:12
  162.2 13.2 %all_gather.46 = bf16[512,256]{0,1:T(8,128)(2,1)S(1)} all-gather(bf16[512,128]{0,1:T(8,128)(2,1)S(1)} %multiply_convert_fusion.8), channel_id=1, replica_groups=mesh['tm'=256,'chan'=2] {'chan'}, dimensions={1}, use_global_device_ids=true | all-gather | bytes 393216 | tf_op jit(solution)/shard_map/all_gather | solution.py:130
  179.2 13.5 %all_gather.47 = f32[4,256]{0,1:T(8,128)S(1)} all-gather(f32[4,128]{0,1:T(8,128)S(1)} %broadcast_divide_fusion), channel_id=1, replica_groups=mesh['tm'=256,'chan'=2] {'chan'}, dimensions={1}, use_global_device_ids=true | all-gather | bytes 6144 | tf_op jit(solution)/shard_map/all_gather | solution.py:146
  199.0 13.2 %all_gather.48 = bf16[512,256]{0,1:T(8,128)(2,1)S(1)} all-gather(bf16[512,128]{0,1:T(8,128)(2,1)S(1)} %fusion.13), channel_id=1, replica_groups=mesh['tm'=256,'chan'=2] {'chan'}, dimensions={1}, use_global_device_ids=true | all-gather | bytes 393216 | tf_op jit(solution)/shard_map/all_gather | solution.py:155
  215.0 7.6 %collective-permute-done.4 = bf16[512,256]{0,1:T(8,128)(2,1)S(1)} collective-permute-done((bf16[512,256]{0,1:T(8,128)(2,1)S(1)}, bf16[512,256]{0,1:T(8,128)(2,1)S(1)}, u32[]{:S(2)}, u32[]{:S(2)}) %collective-permute-start.4) | collective-permute-done | bytes 262176 | tf_op jit(solution)/shard_map/ppermute | solution.py:12
  223.9 60.6 %reduce-scatter.13.cloned.1.call-done = bf16[128,512]{1,0:T(8,128)(2,1)} async-done(((bf16[256,512]{1,0:T(8,128)(2,1)}), bf16[128,512]{1,0:T(8,128)(2,1)}) %reduce-scatter.13.cloned.1.call-update) | async-done | bytes 131088
  285.5 14.0 %all_gather.49 = bf16[512,256]{1,0:T(8,128)(2,1)S(1)} all-gather(bf16[512,128]{1,0:T(8,128)(2,1)S(1)} %copy.38), channel_id=1, replica_groups=mesh['tm'=256,'chan'=2] {'chan'}, dimensions={1}, use_global_device_ids=true | all-gather | bytes 393216 | tf_op jit(solution)/shard_map/all_gather | solution.py:165
  301.7 5.5 %collective-permute-done.5 = bf16[512,256]{0,1:T(8,128)(2,1)S(1)} collective-permute-done((bf16[512,256]{0,1:T(8,128)(2,1)S(1)}, bf16[512,256]{0,1:T(8,128)(2,1)S(1)}, u32[]{:S(2)}, u32[]{:S(2)}) %collective-permute-start.5) | collective-permute-done | bytes 262176 | tf_op jit(solution)/shard_map/ppermute | solution.py:12
  308.5 41.2 %reduce-scatter.15.cloned.1.call-done = bf16[128,512]{1,0:T(8,128)(2,1)} async-done(((bf16[256,512]{1,0:T(8,128)(2,1)}), bf16[128,512]{1,0:T(8,128)(2,1)}) %reduce-scatter.15.cloned.1.call-update) | async-done | bytes 131088
  350.7 14.0 %all_gather.50 = bf16[512,256]{1,0:T(8,128)(2,1)S(1)} all-gather(bf16[512,128]{1,0:T(8,128)(2,1)S(1)} %add_convert_fusion.2), channel_id=1, replica_groups=mesh['tm'=256,'chan'=2] {'chan'}, dimensions={1}, use_global_device_ids=true | all-gather | bytes 393216 | tf_op jit(solution)/shard_map/all_gather | solution.py:165
  366.9 7.0 %collective-permute-done.6 = bf16[512,256]{0,1:T(8,128)(2,1)S(1)} collective-permute-done((bf16[512,256]{0,1:T(8,128)(2,1)S(1)}, bf16[512,256]{0,1:T(8,128)(2,1)S(1)}, u32[]{:S(2)}, u32[]{:S(2)}) %collective-permute-start.6) | collective-permute-done | bytes 262176 | tf_op jit(solution)/shard_map/ppermute | solution.py:12
  375.2 42.1 %reduce-scatter.17.cloned.1.call-done = bf16[128,512]{1,0:T(8,128)(2,1)} async-done(((bf16[256,512]{1,0:T(8,128)(2,1)}), bf16[128,512]{1,0:T(8,128)(2,1)}) %reduce-scatter.17.cloned.1.call-update) | async-done | bytes 131088
  418.4 14.0 %all_gather.51 = bf16[512,256]{1,0:T(8,128)(2,1)S(1)} all-gather(bf16[512,128]{1,0:T(8,128)(2,1)S(1)} %add_convert_fusion.1), channel_id=1, replica_groups=mesh['tm'=256,'chan'=2] {'chan'}, dimensions={1}, use_global_device_ids=true | all-gather | bytes 393216 | tf_op jit(solution)/shard_map/all_gather | solution.py:165
  434.4 5.5 %collective-permute-done.7 = bf16[512,256]{0,1:T(8,128)(2,1)S(1)} collective-permute-done((bf16[512,256]{0,1:T(8,128)(2,1)S(1)}, bf16[512,256]{0,1:T(8,128)(2,1)S(1)}, u32[]{:S(2)}, u32[]{:S(2)}) %collective-permute-start.7) | collective-permute-done | bytes 262176 | tf_op jit(solution)/shard_map/ppermute | solution.py:12
  441.7 42.4 %reduce-scatter.19.cloned.1.call-done = bf16[128,512]{1,0:T(8,128)(2,1)} async-done(((bf16[256,512]{1,0:T(8,128)(2,1)}), bf16[128,512]{1,0:T(8,128)(2,1)}) %reduce-scatter.19.cloned.1.call-update) | async-done | bytes 131088
  (157 shorter events, 55.3 us)
Async XLA Ops:
  7.2 185.5 %copy-start = (f32[256,256]{1,0:T(8,128)S(1)}, f32[256,256]{1,0:T(8,128)}, u32[]{:S(2)}) copy-start(f32[256,256]{1,0:T(8,128)} %param.19) | copy-start | bytes 786436
  7.2 277.3 %reduce-scatter.13.cloned.1.call-start = ((), (), s32[]{:S(2)}) async-start(), calls=%async_computation.4 | async-start | bytes 393216
  26.8 12.6 %collective-permute-start = (bf16[512,256]{1,0:T(8,128)(2,1)S(1)}, bf16[512,256]{1,0:T(8,128)(2,1)}, u32[]{:S(2)}, u32[]{:S(2)}) collective-permute-start(bf16[512,256]{1,0:T(8,128)(2,1)S(1)} %all_gather.39), channel_id=1, source_target_pairs={{0,32},{2,34},{4,36},{6,38},{8,40},{10,42},{12,44},{14,46},{16,48}... | collective-permute-start | bytes 786440 | tf_op jit(solution)/shard_map/ppermute | solution.py:12
  33.4 142.1 %copy-start.22 = (f32[512]{0:T(512)}, f32[512]{0:T(512)S(1)}, u32[]{:S(2)}) copy-start(f32[512]{0:T(512)S(1)} %fusion.97) | copy-start | bytes 6148
  38.0 137.5 %copy-start.20 = (bf16[1,256,256]{2,1,0:T(8,128)(2,1)}, bf16[1,256,256]{2,1,0:T(8,128)(2,1)S(1)}, u32[]{:S(2)}) copy-start(bf16[1,256,256]{2,1,0:T(8,128)(2,1)S(1)} %get-tuple-element.20) | copy-start | bytes 393220
  38.4 45.7 %copy-start.2 = (bf16[256,128]{1,0:T(8,128)(2,1)}, bf16[256,128]{1,0:T(8,128)(2,1)S(1)}, u32[]{:S(2)}) copy-start(bf16[256,128]{1,0:T(8,128)(2,1)S(1)} %get-tuple-element.62) | copy-start | bytes 196612
  38.4 45.7 %copy-start.4 = (bf16[256,128]{1,0:T(8,128)(2,1)}, bf16[256,128]{1,0:T(8,128)(2,1)S(1)}, u32[]{:S(2)}) copy-start(bf16[256,128]{1,0:T(8,128)(2,1)S(1)} %get-tuple-element.63) | copy-start | bytes 196612
  75.4 8.7 %collective-permute-start.1 = (bf16[512,256]{1,0:T(8,128)(2,1)S(1)}, bf16[512,256]{1,0:T(8,128)(2,1)S(1)}, u32[]{:S(2)}, u32[]{:S(2)}) collective-permute-start(bf16[512,256]{1,0:T(8,128)(2,1)S(1)} %all_gather.41), channel_id=1, source_target_pairs={{0,64},{2,66},{4,68},{6,70},{8,72},{10,74},{12,76},{14,78},{16,80}... | collective-permute-start | bytes 786440 | tf_op jit(solution)/shard_map/ppermute | solution.py:12
  111.9 8.4 %collective-permute-start.2 = (bf16[512,256]{1,0:T(8,128)(2,1)S(1)}, bf16[512,256]{1,0:T(8,128)(2,1)S(1)}, u32[]{:S(2)}, u32[]{:S(2)}) collective-permute-start(bf16[512,256]{1,0:T(8,128)(2,1)S(1)} %all_gather.43), channel_id=1, source_target_pairs={{0,128},{2,130},{4,132},{6,134},{8,136},{10,138},{12,140},{14,142}... | collective-permute-start | bytes 786440 | tf_op jit(solution)/shard_map/ppermute | solution.py:12
  117.2 41.3 %copy-start.17 = (bf16[1,256,256]{2,1,0:T(8,128)(2,1)S(1)}, bf16[1,256,256]{2,1,0:T(8,128)(2,1)}, u32[]{:S(2)}) copy-start(bf16[1,256,256]{2,1,0:T(8,128)(2,1)} %get-tuple-element.23) | copy-start | bytes 393220
  152.6 9.2 %collective-permute-start.3 = (bf16[512,256]{1,0:T(8,128)(2,1)S(1)}, bf16[512,256]{1,0:T(8,128)(2,1)S(1)}, u32[]{:S(2)}, u32[]{:S(2)}) collective-permute-start(bf16[512,256]{1,0:T(8,128)(2,1)S(1)} %all_gather.45), channel_id=1, source_target_pairs={{0,256},{2,258},{4,260},{6,262},{8,264},{10,266},{12,268},{14,270}... | collective-permute-start | bytes 786440 | tf_op jit(solution)/shard_map/ppermute | solution.py:12
  213.3 86.2 %copy-start.12 = (bf16[1,256,256]{2,1,0:T(8,128)(2,1)S(1)}, bf16[1,256,256]{2,1,0:T(8,128)(2,1)}, u32[]{:S(2)}) copy-start(bf16[1,256,256]{2,1,0:T(8,128)(2,1)} %get-tuple-element.24) | copy-start | bytes 393220
  213.3 86.4 %copy-start.18 = (bf16[1,256,256]{2,1,0:T(8,128)(2,1)S(1)}, bf16[1,256,256]{2,1,0:T(8,128)(2,1)}, u32[]{:S(2)}) copy-start(bf16[1,256,256]{2,1,0:T(8,128)(2,1)} %get-tuple-element.23) | copy-start | bytes 393220
  213.3 9.3 %collective-permute-start.4 = (bf16[512,256]{0,1:T(8,128)(2,1)S(1)}, bf16[512,256]{0,1:T(8,128)(2,1)S(1)}, u32[]{:S(2)}, u32[]{:S(2)}) collective-permute-start(bf16[512,256]{0,1:T(8,128)(2,1)S(1)} %pad_maximum_fusion), channel_id=1, source_target_pairs={{256,0},{258,2},{260,4},{262,6},{264,8},{266,10},{268,12},{270,14}... | collective-permute-start | bytes 786440 | tf_op jit(solution)/shard_map/ppermute | solution.py:12
  223.8 125.8 %reduce-scatter.15.cloned.1.call-start = ((), (), s32[]{:S(2)}) async-start(), calls=%async_computation.5 | async-start | bytes 393216
  300.0 64.7 %copy-start.10 = (bf16[1,256,256]{2,1,0:T(8,128)(2,1)S(1)}, bf16[1,256,256]{2,1,0:T(8,128)(2,1)}, u32[]{:S(2)}) copy-start(bf16[1,256,256]{2,1,0:T(8,128)(2,1)} %get-tuple-element.26) | copy-start | bytes 393220
  300.0 64.9 %copy-start.16 = (bf16[1,256,256]{2,1,0:T(8,128)(2,1)S(1)}, bf16[1,256,256]{2,1,0:T(8,128)(2,1)}, u32[]{:S(2)}) copy-start(bf16[1,256,256]{2,1,0:T(8,128)(2,1)} %get-tuple-element.21) | copy-start | bytes 393220
  300.0 7.2 %collective-permute-start.5 = (bf16[512,256]{0,1:T(8,128)(2,1)S(1)}, bf16[512,256]{0,1:T(8,128)(2,1)S(1)}, u32[]{:S(2)}, u32[]{:S(2)}) collective-permute-start(bf16[512,256]{0,1:T(8,128)(2,1)S(1)} %pad_maximum_fusion.1), channel_id=1, source_target_pairs={{128,0},{130,2},{132,4},{134,6},{136,8},{138,10},{140,12},{142,14}... | collective-permute-start | bytes 786440 | tf_op jit(solution)/shard_map/ppermute | solution.py:12
  308.4 108.9 %reduce-scatter.17.cloned.1.call-start = ((), (), s32[]{:S(2)}) async-start(), calls=%async_computation.6 | async-start | bytes 393216
  365.2 67.1 %copy-start.8 = (bf16[1,256,256]{2,1,0:T(8,128)(2,1)S(1)}, bf16[1,256,256]{2,1,0:T(8,128)(2,1)}, u32[]{:S(2)}) copy-start(bf16[1,256,256]{2,1,0:T(8,128)(2,1)} %get-tuple-element.25) | copy-start | bytes 393220
  365.2 67.3 %copy-start.14 = (bf16[1,256,256]{2,1,0:T(8,128)(2,1)S(1)}, bf16[1,256,256]{2,1,0:T(8,128)(2,1)}, u32[]{:S(2)}) copy-start(bf16[1,256,256]{2,1,0:T(8,128)(2,1)} %get-tuple-element.22) | copy-start | bytes 393220
  365.2 8.8 %collective-permute-start.6 = (bf16[512,256]{0,1:T(8,128)(2,1)S(1)}, bf16[512,256]{0,1:T(8,128)(2,1)S(1)}, u32[]{:S(2)}, u32[]{:S(2)}) collective-permute-start(bf16[512,256]{0,1:T(8,128)(2,1)S(1)} %pad_maximum_fusion.2), channel_id=1, source_target_pairs={{64,0},{66,2},{68,4},{70,6},{72,8},{74,10},{76,12},{78,14},{80,16}... | collective-permute-start | bytes 786440 | tf_op jit(solution)/shard_map/ppermute | solution.py:12
  375.1 109.0 %reduce-scatter.19.cloned.1.call-start = ((), (), s32[]{:S(2)}) async-start(), calls=%async_computation.7 | async-start | bytes 393216
  432.8 7.1 %collective-permute-start.7 = (bf16[512,256]{0,1:T(8,128)(2,1)S(1)}, bf16[512,256]{0,1:T(8,128)(2,1)S(1)}, u32[]{:S(2)}, u32[]{:S(2)}) collective-permute-start(bf16[512,256]{0,1:T(8,128)(2,1)S(1)} %pad_maximum_fusion.3), channel_id=1, source_target_pairs={{32,0},{34,2},{36,4},{38,6},{40,8},{42,10},{44,12},{46,14},{48,16}... | collective-permute-start | bytes 786440 | tf_op jit(solution)/shard_map/ppermute | solution.py:12
  (12 other events, 239.2 us)
Sparse Core Ops, SparseCore 0:
  223.9 60.5 reduce-scatter.12
  308.5 41.0 reduce-scatter.14
  375.3 41.9 reduce-scatter.16
  441.2 42.8 reduce-scatter.18
where the time goes:
time: 493 us; the launch traced here: 492 us
  waiting for transfers between devices  222 us (45%)
  blocking collectives  194 us (39%)
  starting transfers between devices  23.4 us (5%)
  between operations  15.2 us (3%)
  local copies, waits for them, and re-layouts  15.1 us (3%)
  matrix products  12.6 us (3%)
  other arithmetic  9.65 us (2%)
    unnamed x8, waiting for transfers between devices  186 us
    all_gather x4, blocking collectives, local(): whole = lax.all_gather(current, 'chan', axis=1, tiled=True)  72 us
    all_gather x4, blocking collectives, local(): gated_all = lax.all_gather(gated, 'chan', axis=1, tiled=True)  53.9 us
    all_gather x3, blocking collectives, local(): rows_all = lax.all_gather(grad_rows, 'chan', axis=1, tiled=True)  41.9 us
    ppermute x8, waiting for transfers between devices, passed_along(): return lax.ppermute(block, axis, route)  35.6 us
    ppermute x8, starting transfers between devices, passed_along(): return lax.ppermute(block, axis, route)  23.3 us
    all_gather x1, blocking collectives, local(): pooled = lax.all_gather(pooled_part, 'chan', axis=1, tiled=True)  13.5 us
    all_gather x1, blocking collectives, local(): skip_grads_all = lax.all_gather(grad_skip, 'chan', axis=1, tiled=True)  13.2 us
  transfers between devices with their start and end apart: 12, of which 11 were waited for; matrix products, arithmetic and copies ran while one was open for 2% of the time, Pallas kernels for 0%

commit v1 on v0

v1 whole, which is shorter than its diff:
```python
import jax
import jax.numpy as jnp
from jax import lax
from jax.experimental import pallas as pl
from jax.experimental.pallas import tpu as pltpu
from jax.sharding import Mesh
from jax.sharding import PartitionSpec as P

WLEN = 128
FIRST_DILATION = 8192
F32 = jnp.float32
BF16 = jnp.bfloat16
EXACT = lax.Precision.HIGHEST


def dot(a, b):
    return jnp.dot(a, b, preferred_element_type=F32)


def dot_t(a, b, precision=None):
    return lax.dot_general(
        a, b, (((1,), (1,)), ((), ())), preferred_element_type=F32, precision=precision
    )


def sigmoid(v):
    return 0.5 * jnp.tanh(0.5 * v) + 0.5


def row_keep(limit, base, blocks, chunk, width):
    rows = lax.broadcasted_iota(jnp.int32, (blocks * chunk, width), 0)
    position = (rows // chunk) * FIRST_DILATION + rows % chunk + base
    return position < limit


def forward_kernel(
    blocks,
    chunk,
    place_ref,
    bin_ref,
    seen_ref,
    both_ref,
    tap_ref,
    bias_ref,
    res_ref,
    skipw_ref,
    tanh_ref,
    gate_ref,
    skip_ref,
    pool_ref,
):
    layers = tap_ref.shape[0]
    part = both_ref.shape[2] // 2
    width = 2 * part
    rows = blocks * chunk
    limit, base, chan_at = place_ref[0], place_ref[1], place_ref[2]
    whole = both_ref[...].reshape(2, rows, 2 * part)
    current = jnp.concatenate([whole[0, :, :part], whole[1, :, :part]], axis=1)
    skip_sum = jnp.concatenate([whole[0, :, part:], whole[1, :, part:]], axis=1).astype(F32)
    for layer in range(layers):
        late = chunk * 2**layer
        delayed = jnp.concatenate(
            [jnp.zeros((late, width), BF16), current[: rows - late]], axis=0
        )
        preact = (
            dot(delayed, tap_ref[layer, 0])
            + dot(current, tap_ref[layer, 1])
            + bias_ref[layer : layer + 1, :]
        )
        filters = jnp.tanh(preact[:, :width])
        gates = sigmoid(preact[:, width:])
        tanh_ref[layer] = filters
        gate_ref[layer] = gates
        gated = (filters * gates).astype(BF16)
        if layer < layers - 1:
            current = (current.astype(F32) + dot(gated, res_ref[layer])).astype(BF16)
        skip_sum = skip_sum + dot(gated, skipw_ref[layer])
    skip_ref[...] = skip_sum
    keep = row_keep(limit, base, blocks, chunk, width)
    active = jnp.where(keep, skip_sum * sigmoid(skip_sum), 0.0)
    sums = active.reshape(blocks, chunk, width).sum(axis=1)
    first = 2 * chan_at
    line = lax.broadcasted_iota(jnp.int32, (8, width), 0)
    extra = jnp.where(
        line == 0,
        bin_ref[first].astype(F32),
        jnp.where(
            line == 1,
            bin_ref[first + 1].astype(F32),
            jnp.where(line == 2, seen_ref[first].astype(F32), seen_ref[first + 1].astype(F32)),
        ),
    )
    for other in range(blocks):
        pool_ref[other, :blocks, :] = sums
        pool_ref[other, blocks:, :] = extra


def mixture(params, log_time, seen, mixes):
    lanes = params.shape[1]
    lane = lax.broadcasted_iota(jnp.int32, params.shape, 1)
    valid = lane < mixes
    bend_logit = jnp.tanh(params)
    log_scale = jnp.tanh(pltpu.roll(params, lanes - mixes, 1))
    bend_shape = jnp.tanh(pltpu.roll(params, lanes - 2 * mixes, 1))
    logits = 4.0 * bend_logit
    raised = jnp.where(valid, jnp.exp(logits), 0.0)
    total = jnp.sum(raised, axis=1, keepdims=True)
    log_weight = logits - jnp.log(total)
    log_shape = 0.5 * bend_shape
    shape = jnp.exp(log_shape)
    ratio = log_time - log_scale
    power = jnp.exp(shape * ratio)
    density = log_shape - log_scale + (shape - 1.0) * ratio - power
    component = jnp.where(seen, density, -power)
    likely = jnp.where(valid, jnp.exp(log_weight + component), 0.0)
    mass = jnp.sum(likely, axis=1, keepdims=True)
    nll = -jnp.log(mass)
    owned = likely / mass
    to_logit = (raised / total - owned) * 4.0 * (1.0 - bend_logit * bend_logit)
    steep = power * shape
    to_scale = jnp.where(seen, steep - shape, steep)
    to_shape = jnp.where(seen, 1.0 + shape * ratio, 0.0) - steep * ratio
    to_scale = -owned * to_scale * (1.0 - log_scale * log_scale)
    to_shape = -owned * to_shape * 0.5 * (1.0 - bend_shape * bend_shape)
    zero = jnp.zeros_like(params)
    grad = (
        jnp.where(valid, to_logit, zero)
        + pltpu.roll(jnp.where(valid, to_scale, zero), mixes, 1)
        + pltpu.roll(jnp.where(valid, to_shape, zero), 2 * mixes, 1)
    )
    return nll, grad


def backward_kernel(
    blocks,
    chunk,
    place_ref,
    pool_ref,
    tanh_ref,
    gate_ref,
    skip_ref,
    tap_ref,
    res_ref,
    skipw_ref,
    head1_ref,
    headb1_ref,
    head2_ref,
    headb2_ref,
    nll_ref,
    grad_ref,
    pad_ref,
):
    layers = tap_ref.shape[0]
    width = skip_ref.shape[1]
    part = width // 2
    rows = blocks * chunk
    lanes = pad_ref.shape[1]
    outs = head2_ref.shape[1]
    limit, base, chan_at, block_at, shard_base = (place_ref[i] for i in range(5))
    half = blocks // 2
    received = pool_ref[...]
    sums = jnp.concatenate(
        [
            received[:half, :blocks, :].sum(axis=0),
            received[half:, :blocks, :].sum(axis=0),
        ],
        axis=0,
    )
    bins = jnp.concatenate([received[:, blocks, :lanes], received[:, blocks + 1, :lanes]], axis=0)
    seen = (
        jnp.concatenate(
            [received[:, blocks + 2, :lanes], received[:, blocks + 3, :lanes]], axis=0
        )
        == 1.0
    )
    log_time = jnp.log((bins + 1.0) / 8.0)
    window = lax.broadcasted_iota(jnp.int32, (2 * blocks, width), 0)
    start = (
        (window % blocks) * FIRST_DILATION
        + shard_base
        + (2 * chan_at + window // blocks) * WLEN
    )
    count = jnp.clip(limit - start, 1, WLEN).astype(F32)
    pooled = sums / count
    pad_ref[...] = jnp.zeros_like(pad_ref)
    pad_ref[:width, :outs] = head2_ref[...]
    pad_ref[width : width + 1, :outs] = headb2_ref[...]
    head2 = pad_ref[:width, :]
    inner = (
        jnp.dot(pooled, head1_ref[...], preferred_element_type=F32, precision=EXACT)
        + headb1_ref[...]
    )
    open_inner = sigmoid(inner)
    hidden = inner * open_inner
    params = (
        jnp.dot(hidden, head2, preferred_element_type=F32, precision=EXACT)
        + pad_ref[width : width + 1, :]
    )
    nll, to_params = mixture(params, log_time, seen, outs // 3)
    to_hidden = dot_t(to_params, head2, EXACT)
    to_inner = to_hidden * open_inner * (1.0 + inner * (1.0 - open_inner))
    to_pooled = dot_t(to_inner, head1_ref[...], EXACT)

    row = lax.broadcasted_iota(jnp.int32, (2 * blocks, 2), 0)
    col = lax.broadcasted_iota(jnp.int32, (2 * blocks, 2), 1)
    mine = row == col * blocks + block_at
    nll_ref[...] = jnp.sum(jnp.where(mine, nll, 0.0), axis=0, keepdims=True)

    own_pool = jnp.where(block_at < half, to_pooled[:blocks], to_pooled[blocks:])
    spread = jnp.broadcast_to(own_pool[:, None, :], (blocks, chunk, width)).reshape(rows, width)
    keep = row_keep(limit, base, blocks, chunk, width)
    skip_sum = skip_ref[...]
    sig = sigmoid(skip_sum)
    slope = sig * (1.0 + skip_sum * (1.0 - sig))
    grad_skip = jnp.where(keep, spread * slope, 0.0).astype(BF16)
    grad_rows = None
    for layer in range(layers - 1, -1, -1):
        early = chunk * 2**layer
        grad_gated = dot_t(grad_skip, skipw_ref[layer])
        if grad_rows is not None:
            grad_gated = grad_gated + dot_t(grad_rows, res_ref[layer])
        filters = tanh_ref[layer]
        gates = gate_ref[layer]
        through = grad_gated * gates
        to_filter = (through * (1.0 - filters * filters)).astype(BF16)
        to_gate = (through * filters * (1.0 - gates)).astype(BF16)
        preact_grad = jnp.concatenate([to_filter, to_gate], axis=1)
        ahead = jnp.concatenate(
            [preact_grad[early:], jnp.zeros((early, 2 * width), BF16)], axis=0
        )
        summed = dot_t(preact_grad, tap_ref[layer, 1]) + dot_t(ahead, tap_ref[layer, 0])
        if grad_rows is not None:
            summed = summed + grad_rows.astype(F32)
        grad_rows = summed.astype(BF16)
    grad_ref[0] = grad_rows[:, :part].reshape(blocks, chunk, part)
    grad_ref[1] = grad_rows[:, part:].reshape(blocks, chunk, part)


def local(
    signal,
    skip_in,
    tap_weight,
    tap_bias,
    res_weight,
    skip_weight,
    head_w1,
    head_b1,
    head_w2,
    head_second_bias,
    event_bin,
    observed,
    valid_len,
):
    blocks = lax.axis_size("blk")
    chans = lax.axis_size("chan")
    shard_rows, part = signal.shape
    width = part * chans
    peers = blocks * chans
    chunk = shard_rows // peers
    rows = blocks * chunk
    layers = tap_weight.shape[0]
    block_at = lax.axis_index("blk")
    chan_at = lax.axis_index("chan")
    shard_base = lax.axis_index("j") * shard_rows
    base = shard_base + (chan_at * blocks + block_at) * chunk
    place = jnp.stack([valid_len[0], base, chan_at, block_at, shard_base]).astype(jnp.int32)

    both = jnp.concatenate(
        [signal.reshape(peers, chunk, part), skip_in.reshape(peers, chunk, part)], axis=2
    )
    both = lax.all_to_all(both, ("chan", "blk"), 0, 0, tiled=True)

    vmem = pl.BlockSpec(memory_space=pltpu.VMEM)
    smem = pl.BlockSpec(memory_space=pltpu.SMEM)
    shape = jax.ShapeDtypeStruct
    filters, gates, skip_sum, pool = pl.pallas_call(
        lambda *refs: forward_kernel(blocks, chunk, *refs),
        out_shape=(
            shape((layers, rows, width), F32),
            shape((layers, rows, width), F32),
            shape((rows, width), F32),
            shape((blocks, blocks + 8, width), F32),
        ),
        in_specs=[smem, smem, smem] + [vmem] * 5,
        out_specs=(vmem,) * 4,
        compiler_params=pltpu.CompilerParams(vmem_limit_bytes=32 << 20),
        name="forward",
    )(place, event_bin, observed, both, tap_weight, tap_bias, res_weight, skip_weight)

    pool = lax.all_to_all(pool, "blk", 0, 0, tiled=True)

    nll, grads = pl.pallas_call(
        lambda *refs: backward_kernel(blocks, chunk, *refs),
        out_shape=(
            shape((1, 2), F32),
            shape((chans, blocks, chunk, part), BF16),
        ),
        in_specs=[smem] + [vmem] * 11,
        out_specs=(vmem, vmem),
        scratch_shapes=[pltpu.VMEM((width + 8, 128), F32)],
        compiler_params=pltpu.CompilerParams(vmem_limit_bytes=32 << 20),
        name="backward",
    )(
        place,
        pool,
        filters,
        gates,
        skip_sum,
        tap_weight,
        res_weight,
        skip_weight,
        head_w1,
        head_b1.reshape(1, -1),
        head_w2,
        head_second_bias.reshape(1, -1),
    )
    grads = lax.all_to_all(
        grads.reshape(peers, chunk, part), ("chan", "blk"), 0, 0, tiled=True
    )
    return (nll.reshape(2), grads.reshape(shard_rows, part))


def solution(mesh):
    blocks = 16
    devices = mesh.devices
    split = Mesh(
        devices.reshape(blocks, devices.shape[0] // blocks, devices.shape[1]),
        ("blk", "j", "chan"),
    )
    time = ("blk", "j")
    return jax.shard_map(
        local,
        mesh=split,
        in_specs=(
            P(time, "chan"),
            P(time, "chan"),
            P(),
            P(),
            P(),
            P(),
            P(),
            P(),
            P(),
            P(),
            P(time),
            P(time),
            P(),
        ),
        out_specs=(P(("blk", "j", "chan")), P(time, "chan")),
        check_vma=False,
    )
```

time: 493 us -> 103 us (0.21)
  the two profiles are of different devices: /device:TPU:1 before, /device:TPU:32 now
where the time goes in v1:
time: 103 us; the launch traced here: 102 us
  waiting for transfers between devices  34 us (33%)
  starting transfers between devices  23.3 us (23%)
  blocking collectives  20.5 us (20%)
  local copies, waits for them, and re-layouts  15 us (15%)
  Pallas kernels  6.68 us (6%)
  other arithmetic  1.71 us (2%)
  between operations  1.37 us (1%)
    all_to_all x1, waiting for transfers between devices, local(): both = lax.all_to_all(both, ('chan', 'blk'), 0, 0, tiled=True)  25.4 us
    all_to_all x1, blocking collectives, local(): lax.all_to_all(grads.reshape(peers, chunk, part), ('chan', 'blk'), 0, 0,...  20.5 us
    all_to_all x1, starting transfers between devices, local(): both = lax.all_to_all(both, ('chan', 'blk'), 0, 0, tiled=True)  19.7 us
    unnamed x40, local copies, waits for them, and re-layouts  14.9 us
    all_to_all x1, waiting for transfers between devices, local(): pool = lax.all_to_all(pool, 'blk', 0, 0, tiled=True)  8.56 us
    pallas_call x1, Pallas kernels, local(): pl.pallas_call(lambda *refs: backward_kernel(blocks, chunk, *refs), out_s...  4.53 us
    all_to_all x1, starting transfers between devices, local(): pool = lax.all_to_all(pool, 'blk', 0, 0, tiled=True)  3.59 us
    pallas_call x1, Pallas kernels, local(): pl.pallas_call(lambda *refs: forward_kernel(blocks, chunk, *refs), out_sh...  2.15 us
  transfers between devices with their start and end apart: 2, of which 2 were waited for; matrix products, arithmetic and copies ran while one was open for 1% of the time, Pallas kernels for 0%

profile of v1, /device:TPU:32, one launch (start us, length us, event | category | flops | bytes accessed | tf_op | source)
XLA Modules:
  0.0 102.5 jit_solution(8589698457813371037)
XLA Ops:
  0.6 1.7 %pad_maximum_fusion = bf16[32,16,256]{2,1,0:T(8,128)(2,1)} fusion(bf16[32,16,128]{2,1,0:T(8,128)(2,1)} %bitcast.15, bf16[32,16,128]{2,1,0:T(8,128)(2,1)} %bitcast.16), kind=kLoop, calls=%fused_computation | loop fusion | flops 524288 | bytes 524288 | tf_op jit(solution)/shard_map/concatenate | solution.py:268
  2.3 19.7 %all-to-all-start = ((bf16[32,16,256]{2,1,0:T(8,128)(2,1)}), bf16[32,16,256]{2,1,0:T(8,128)(2,1)S(1)}, u32[]{:S(2)}, u32[]{:S(2)}) async-start(bf16[32,16,256]{2,1,0:T(8,128)(2,1)} %pad_maximum_fusion), calls=%async_computation | async-start | bytes 524288 | tf_op jit(solution)/shard_map/all_to_all | solution.py:271
  22.8 25.4 %all-to-all-done.refs_3_ = bf16[32,16,256]{2,1,0:T(8,128)(2,1)S(1)} async-done(((bf16[32,16,256]{2,1,0:T(8,128)(2,1)}), bf16[32,16,256]{2,1,0:T(8,128)(2,1)S(1)}, u32[]{:S(2)}, u32[]{:S(2)}) %all-to-all-start) | async-done | bytes 262176 | tf_op jit(solution)/shard_map/all_to_all | solution.py:271
  48.2 1.6 %copy-done = bf16[4,2,256,512]{3,2,1,0:T(8,128)(2,1)S(1)} copy-done((bf16[4,2,256,512]{3,2,1,0:T(8,128)(2,1)S(1)}, bf16[4,2,256,512]{3,2,1,0:T(8,128)(2,1)}, u32[]{:S(2)}) %copy-start) | copy-done | bytes 2097176
  49.8 1.0 %copy-done.2 = bf16[4,256,256]{2,1,0:T(8,128)(2,1)S(1)} copy-done((bf16[4,256,256]{2,1,0:T(8,128)(2,1)S(1)}, bf16[4,256,256]{2,1,0:T(8,128)(2,1)}, u32[]{:S(2)}) %copy-start.2) | copy-done | bytes 524312
  50.8 1.0 copy-done.4
  51.8 0.7 copy-done.14
  52.5 0.7 copy-done.16
  53.2 0.7 copy-done.17
  53.9 2.2 %forward.1 = (f32[4,256,256]{2,1,0:T(8,128)S(1)}, f32[4,256,256]{2,1,0:T(8,128)S(1)}, f32[256,256]{1,0:T(8,128)S(1)}, f32[16,24,256]{2,1,0:T(8,128)S(1)}) custom-call(s32[5]{0:T(128)S(1)} %stack.19.refs_0_, s32[4]{0:T(128)S(1)} %copy-done.16, s32[4]{0:T(128)S(1)} %copy-done.17, bf16[32,16,256]{2,1,0:T(8,128)(2,1)S(1)} %all-to-all-done.refs_3_, ...), custom_call_target="tpu_custom_call" | custom-call | tf_op jit(solution)/shard_map/forward/pallas_call | solution.py:276
  56.0 1.0 copy-done.6
  57.0 1.0 copy-done.8
  58.0 0.8 copy-done.10
  58.7 0.7 copy-done.12
  59.5 3.6 %all-to-all-start.1 = ((f32[16,24,256]{2,1,0:T(8,128)}), f32[16,24,256]{2,1,0:T(8,128)S(1)}, u32[]{:S(2)}, u32[]{:S(2)}) async-start(f32[16,24,256]{2,1,0:T(8,128)} %copy-done.10), calls=%async_computation.1 | async-start | bytes 786432 | tf_op jit(solution)/shard_map/all_to_all | solution.py:290
  63.1 0.8 copy.15.refs_10_
  63.9 8.6 %all-to-all-done.1.refs_1_ = f32[16,24,256]{2,1,0:T(8,128)S(1)} async-done(((f32[16,24,256]{2,1,0:T(8,128)}), f32[16,24,256]{2,1,0:T(8,128)S(1)}, u32[]{:S(2)}, u32[]{:S(2)}) %all-to-all-start.1) | async-done | bytes 393248 | tf_op jit(solution)/shard_map/all_to_all | solution.py:290
  72.5 1.2 %copy-done.7 = f32[4,256,256]{2,1,0:T(8,128)S(1)} copy-done((f32[4,256,256]{2,1,0:T(8,128)S(1)}, f32[4,256,256]{2,1,0:T(8,128)}, u32[]{:S(2)}) %copy-start.7) | copy-done | bytes 1048600
  73.7 1.2 %copy-done.9 = f32[4,256,256]{2,1,0:T(8,128)S(1)} copy-done((f32[4,256,256]{2,1,0:T(8,128)S(1)}, f32[4,256,256]{2,1,0:T(8,128)}, u32[]{:S(2)}) %copy-start.9) | copy-done | bytes 1048600
  74.9 0.9 copy-done.11
  75.9 0.9 copy-done.13
  76.8 4.5 %backward.1 = (f32[1,2]{1,0:T(1,128)}, bf16[2,16,16,128]{3,2,1,0:T(8,128)(2,1)S(1)}) custom-call(s32[5]{0:T(128)S(1)} %stack.19.refs_0_, f32[16,24,256]{2,1,0:T(8,128)S(1)} %all-to-all-done.1.refs_1_, f32[4,256,256]{2,1,0:T(8,128)S(1)} %copy-done.7, f32[4,256,256]{2,1,0:T(8,128)S(1)} %copy-done.9, f32[256,256]{1,0:T(8,128)S(1)} %copy-done.13, ...), custom_call_target="tpu_custom_call" | custom-call | tf_op jit(solution)/shard_map/backward/pallas_call | solution.py:292
  81.4 20.5 %all_to_all.15 = bf16[32,16,128]{2,1,0:T(8,128)(2,1)S(1)} all-to-all(bf16[32,16,128]{2,1,0:T(8,128)(2,1)S(1)} %bitcast.11), channel_id=1, replica_groups=mesh['blk'=16,'j'=16,'chan'=2] {'chan','blk'}, dimensions={0} | all-to-all | bytes 262144 | tf_op jit(solution)/shard_map/all_to_all | solution.py:317
  101.8 0.7 copy.18
  (25 shorter events, 0.1 us)
Async XLA Ops:
  2.3 45.9 %all-to-all-start = ((bf16[32,16,256]{2,1,0:T(8,128)(2,1)}), bf16[32,16,256]{2,1,0:T(8,128)(2,1)S(1)}, u32[]{:S(2)}, u32[]{:S(2)}) async-start(bf16[32,16,256]{2,1,0:T(8,128)(2,1)} %pad_maximum_fusion), calls=%async_computation | async-start | bytes 524288 | tf_op jit(solution)/shard_map/all_to_all | solution.py:271
  48.2 1.6 %copy-start = (bf16[4,2,256,512]{3,2,1,0:T(8,128)(2,1)S(1)}, bf16[4,2,256,512]{3,2,1,0:T(8,128)(2,1)}, u32[]{:S(2)}) copy-start(bf16[4,2,256,512]{3,2,1,0:T(8,128)(2,1)} %refs_5_.3) | copy-start | bytes 6291460
  49.8 1.0 %copy-start.2 = (bf16[4,256,256]{2,1,0:T(8,128)(2,1)S(1)}, bf16[4,256,256]{2,1,0:T(8,128)(2,1)}, u32[]{:S(2)}) copy-start(bf16[4,256,256]{2,1,0:T(8,128)(2,1)} %refs_7_.3) | copy-start | bytes 1572868
  50.8 1.0 copy-start.4
  51.8 0.7 copy-start.14
  52.5 0.7 copy-start.16
  53.2 0.7 copy-start.17
  53.8 18.6 %copy-start.1 = (bf16[4,2,256,512]{3,2,1,0:T(8,128)(2,1)S(1)}, bf16[4,2,256,512]{3,2,1,0:T(8,128)(2,1)}, u32[]{:S(2)}) copy-start(bf16[4,2,256,512]{3,2,1,0:T(8,128)(2,1)} %refs_5_.3) | copy-start | bytes 6291460
  53.8 18.6 %copy-start.3 = (bf16[4,256,256]{2,1,0:T(8,128)(2,1)S(1)}, bf16[4,256,256]{2,1,0:T(8,128)(2,1)}, u32[]{:S(2)}) copy-start(bf16[4,256,256]{2,1,0:T(8,128)(2,1)} %refs_7_.3) | copy-start | bytes 1572868
  53.8 18.6 %copy-start.5 = (bf16[3,256,256]{2,1,0:T(8,128)(2,1)S(1)}, bf16[3,256,256]{2,1,0:T(8,128)(2,1)}, u32[]{:S(2)}) copy-start(bf16[3,256,256]{2,1,0:T(8,128)(2,1)} %refs_6_.3) | copy-start | bytes 1179652
  53.9 18.6 %copy-start.15 = (f32[256]{0:T(256)S(1)}, f32[256]{0:T(256)}, u32[]{:S(2)}) copy-start(f32[256]{0:T(256)} %param.20) | copy-start | bytes 3076
  53.9 18.6 %copy-start.18 = (f32[12]{0:T(128)S(1)}, f32[12]{0:T(128)}, u32[]{:S(2)}) copy-start(f32[12]{0:T(128)} %param.22) | copy-start | bytes 148
  56.0 1.0 copy-start.6
  57.0 1.0 copy-start.8
  58.0 0.8 copy-start.10
  58.7 0.7 copy-start.12
  59.5 13.0 %all-to-all-start.1 = ((f32[16,24,256]{2,1,0:T(8,128)}), f32[16,24,256]{2,1,0:T(8,128)S(1)}, u32[]{:S(2)}, u32[]{:S(2)}) async-start(f32[16,24,256]{2,1,0:T(8,128)} %copy-done.10), calls=%async_computation.1 | async-start | bytes 786432 | tf_op jit(solution)/shard_map/all_to_all | solution.py:290
  72.5 1.2 %copy-start.7 = (f32[4,256,256]{2,1,0:T(8,128)S(1)}, f32[4,256,256]{2,1,0:T(8,128)}, u32[]{:S(2)}) copy-start(f32[4,256,256]{2,1,0:T(8,128)} %copy-done.6) | copy-start | bytes 3145732
  73.7 1.2 %copy-start.9 = (f32[4,256,256]{2,1,0:T(8,128)S(1)}, f32[4,256,256]{2,1,0:T(8,128)}, u32[]{:S(2)}) copy-start(f32[4,256,256]{2,1,0:T(8,128)} %copy-done.8) | copy-start | bytes 3145732
  74.9 0.9 copy-start.11
  75.9 0.9 copy-start.13

commit v2 on v1

--- a/solution.py
+++ b/solution.py
@@ -33,31 +33,85 @@
     return position < limit
 
 
+def start_all(copies):
+    for copy in copies:
+        copy.start()
+
+
+def wait_all(copies):
+    for copy in copies:
+        copy.wait()
+
+
+def join_kernel(signal_ref, skip_ref, both_ref, sems):
+    copies = [
+        pltpu.make_async_copy(signal_ref, both_ref.at[:, 0], sems.at[0]),
+        pltpu.make_async_copy(skip_ref, both_ref.at[:, 1], sems.at[1]),
+    ]
+    start_all(copies)
+    wait_all(copies)
+
+
 def forward_kernel(
     blocks,
     chunk,
     place_ref,
-    bin_ref,
-    seen_ref,
     both_ref,
+    tap_hbm,
+    bias_hbm,
+    res_hbm,
+    skipw_hbm,
+    act_hbm,
+    skip_hbm,
+    pool_hbm,
     tap_ref,
     bias_ref,
     res_ref,
     skipw_ref,
-    tanh_ref,
-    gate_ref,
+    act_ref,
     skip_ref,
     pool_ref,
+    in_sems,
+    out_sems,
 ):
     layers = tap_ref.shape[0]
-    part = both_ref.shape[2] // 2
+    part = both_ref.shape[3]
     width = 2 * part
     rows = blocks * chunk
     limit, base, chan_at = place_ref[0], place_ref[1], place_ref[2]
-    whole = both_ref[...].reshape(2, rows, 2 * part)
-    current = jnp.concatenate([whole[0, :, :part], whole[1, :, :part]], axis=1)
-    skip_sum = jnp.concatenate([whole[0, :, part:], whole[1, :, part:]], axis=1).astype(F32)
+    taps = [
+        pltpu.make_async_copy(tap_hbm.at[k], tap_ref.at[k], in_sems.at[k]) for k in range(layers)
+    ]
+    skips = [
+        pltpu.make_async_copy(skipw_hbm.at[k], skipw_ref.at[k], in_sems.at[layers + k])
+        for k in range(layers)
+    ]
+    ress = [
+        pltpu.make_async_copy(res_hbm.at[k], res_ref.at[k], in_sems.at[2 * layers + k])
+        for k in range(layers - 1)
+    ]
+    bias_copy = pltpu.make_async_copy(bias_hbm, bias_ref, in_sems.at[3 * layers])
+    outs = []
+    start_all([taps[0], bias_copy, ress[0], skips[0]])
+    for k in range(1, layers):
+        start_all([taps[k]] + ress[k : k + 1] + [skips[k]])
+    current = jnp.concatenate(
+        [
+            both_ref[:blocks, 0].reshape(rows, part),
+            both_ref[blocks:, 0].reshape(rows, part),
+        ],
+        axis=1,
+    )
+    skip_sum = jnp.concatenate(
+        [
+            both_ref[:blocks, 1].reshape(rows, part),
+            both_ref[blocks:, 1].reshape(rows, part),
+        ],
+        axis=1,
+    ).astype(F32)
+    bias_copy.wait()
     for layer in range(layers):
+        taps[layer].wait()
         late = chunk * 2**layer
         delayed = jnp.concatenate(
             [jnp.zeros((late, width), BF16), current[: rows - late]], axis=0
@@ -69,30 +123,40 @@
         )
         filters = jnp.tanh(preact[:, :width])
         gates = sigmoid(preact[:, width:])
-        tanh_ref[layer] = filters
-        gate_ref[layer] = gates
+        act_ref[layer, 0] = filters
+        act_ref[layer, 1] = gates
+        outs.append(
+            pltpu.make_async_copy(act_ref.at[layer], act_hbm.at[layer], out_sems.at[layer])
+        )
+        outs[-1].start()
         gated = (filters * gates).astype(BF16)
+        skips[layer].wait()
         if layer < layers - 1:
+            ress[layer].wait()
             current = (current.astype(F32) + dot(gated, res_ref[layer])).astype(BF16)
         skip_sum = skip_sum + dot(gated, skipw_ref[layer])
     skip_ref[...] = skip_sum
+    outs.append(pltpu.make_async_copy(skip_ref, skip_hbm, out_sems.at[layers]))
+    outs[-1].start()
     keep = row_keep(limit, base, blocks, chunk, width)
     active = jnp.where(keep, skip_sum * sigmoid(skip_sum), 0.0)
     sums = active.reshape(blocks, chunk, width).sum(axis=1)
-    first = 2 * chan_at
+    first = 5 + 2 * chan_at
     line = lax.broadcasted_iota(jnp.int32, (8, width), 0)
+    bins = [place_ref[first + i].astype(F32) for i in (0, 1, 4, 5)]
     extra = jnp.where(
         line == 0,
-        bin_ref[first].astype(F32),
-        jnp.where(
-            line == 1,
-            bin_ref[first + 1].astype(F32),
-            jnp.where(line == 2, seen_ref[first].astype(F32), seen_ref[first + 1].astype(F32)),
-        ),
-    )
+        bins[0],
+        jnp.where(line == 1, bins[1], jnp.where(line == 2, bins[2], bins[3])),
+    )
+    sums = sums.astype(BF16)
+    extra = extra.astype(BF16)
     for other in range(blocks):
         pool_ref[other, :blocks, :] = sums
         pool_ref[other, blocks:, :] = extra
+    outs.append(pltpu.make_async_copy(pool_ref, pool_hbm, out_sems.at[layers + 1]))
+    outs[-1].start()
+    wait_all(outs)
 
 
 def mixture(params, log_time, seen, mixes):
@@ -136,29 +200,52 @@
     chunk,
     place_ref,
     pool_ref,
-    tanh_ref,
-    gate_ref,
-    skip_ref,
-    tap_ref,
-    res_ref,
-    skipw_ref,
+    act_hbm,
+    skip_hbm,
+    tap_hbm,
+    res_hbm,
+    skipw_hbm,
     head1_ref,
     headb1_ref,
     head2_ref,
     headb2_ref,
     nll_ref,
     grad_ref,
+    act_ref,
+    skip_ref,
+    tap_ref,
+    res_ref,
+    skipw_ref,
     pad_ref,
+    sems,
 ):
     layers = tap_ref.shape[0]
     width = skip_ref.shape[1]
+    skip_copy = pltpu.make_async_copy(skip_hbm, skip_ref, sems.at[0])
+
+    def loads(k):
+        copies = [
+            pltpu.make_async_copy(skipw_hbm.at[k], skipw_ref.at[k], sems.at[1 + 4 * k]),
+            pltpu.make_async_copy(act_hbm.at[k], act_ref.at[k], sems.at[2 + 4 * k]),
+            pltpu.make_async_copy(tap_hbm.at[k], tap_ref.at[k], sems.at[3 + 4 * k]),
+        ]
+        if k < layers - 1:
+            copies.append(
+                pltpu.make_async_copy(res_hbm.at[k], res_ref.at[k], sems.at[4 + 4 * k])
+            )
+        return copies
+
+    layer_copies = [loads(k) for k in range(layers)]
+    skip_copy.start()
+    for k in range(layers - 1, -1, -1):
+        start_all(layer_copies[k])
     part = width // 2
     rows = blocks * chunk
     lanes = pad_ref.shape[1]
     outs = head2_ref.shape[1]
     limit, base, chan_at, block_at, shard_base = (place_ref[i] for i in range(5))
     half = blocks // 2
-    received = pool_ref[...]
+    received = pool_ref[...].astype(F32)
     sums = jnp.concatenate(
         [
             received[:half, :blocks, :].sum(axis=0),
@@ -209,6 +296,7 @@
     own_pool = jnp.where(block_at < half, to_pooled[:blocks], to_pooled[blocks:])
     spread = jnp.broadcast_to(own_pool[:, None, :], (blocks, chunk, width)).reshape(rows, width)
     keep = row_keep(limit, base, blocks, chunk, width)
+    skip_copy.wait()
     skip_sum = skip_ref[...]
     sig = sigmoid(skip_sum)
     slope = sig * (1.0 + skip_sum * (1.0 - sig))
@@ -216,11 +304,12 @@
     grad_rows = None
     for layer in range(layers - 1, -1, -1):
         early = chunk * 2**layer
+        wait_all(layer_copies[layer])
         grad_gated = dot_t(grad_skip, skipw_ref[layer])
         if grad_rows is not None:
             grad_gated = grad_gated + dot_t(grad_rows, res_ref[layer])
-        filters = tanh_ref[layer]
-        gates = gate_ref[layer]
+        filters = act_ref[layer, 0]
+        gates = act_ref[layer, 1]
         through = grad_gated * gates
         to_filter = (through * (1.0 - filters * filters)).astype(BF16)
         to_gate = (through * filters * (1.0 - gates)).astype(BF16)
@@ -263,56 +352,96 @@
     chan_at = lax.axis_index("chan")
     shard_base = lax.axis_index("j") * shard_rows
     base = shard_base + (chan_at * blocks + block_at) * chunk
-    place = jnp.stack([valid_len[0], base, chan_at, block_at, shard_base]).astype(jnp.int32)
-
-    both = jnp.concatenate(
-        [signal.reshape(peers, chunk, part), skip_in.reshape(peers, chunk, part)], axis=2
-    )
-    both = lax.all_to_all(both, ("chan", "blk"), 0, 0, tiled=True)
-
+    here = jnp.stack([base, chan_at, block_at, shard_base]).astype(jnp.int32)
+    place = jnp.concatenate([valid_len, here, event_bin, observed])
+
+    shape = jax.ShapeDtypeStruct
     vmem = pl.BlockSpec(memory_space=pltpu.VMEM)
     smem = pl.BlockSpec(memory_space=pltpu.SMEM)
-    shape = jax.ShapeDtypeStruct
-    filters, gates, skip_sum, pool = pl.pallas_call(
+    hbm = pl.BlockSpec(memory_space=pltpu.HBM)
+    params = pltpu.CompilerParams(vmem_limit_bytes=24 << 20)
+
+    def stay(array):
+        return pltpu.with_memory_space_constraint(array, pltpu.HBM)
+
+
+    both = pl.pallas_call(
+        join_kernel,
+        out_shape=shape((peers, 2, chunk, part), BF16),
+        in_specs=[hbm, hbm],
+        out_specs=hbm,
+        scratch_shapes=[pltpu.SemaphoreType.DMA((2,))],
+        compiler_params=params,
+        name="join",
+    )(stay(signal.reshape(peers, chunk, part)), stay(skip_in.reshape(peers, chunk, part)))
+    both = lax.all_to_all(both, ("chan", "blk"), 0, 0, tiled=True)
+
+    acts, skip_sum, pool = pl.pallas_call(
         lambda *refs: forward_kernel(blocks, chunk, *refs),
         out_shape=(
-            shape((layers, rows, width), F32),
-            shape((layers, rows, width), F32),
-            shape((rows, width), F32),
-            shape((blocks, blocks + 8, width), F32),
+            pltpu.HBM((layers, 2, rows, width), F32),
+            pltpu.HBM((rows, width), F32),
+            pltpu.HBM((blocks, blocks + 8, width), BF16),
         ),
-        in_specs=[smem, smem, smem] + [vmem] * 5,
-        out_specs=(vmem,) * 4,
-        compiler_params=pltpu.CompilerParams(vmem_limit_bytes=32 << 20),
+        in_specs=[smem, vmem] + [hbm] * 4,
+        out_specs=(hbm,) * 3,
+        scratch_shapes=[
+            pltpu.VMEM(tap_weight.shape, BF16),
+            pltpu.VMEM(tap_bias.shape, F32),
+            pltpu.VMEM(res_weight.shape, BF16),
+            pltpu.VMEM(skip_weight.shape, BF16),
+            pltpu.VMEM((layers, 2, rows, width), F32),
+            pltpu.VMEM((rows, width), F32),
+            pltpu.VMEM((blocks, blocks + 8, width), BF16),
+            pltpu.SemaphoreType.DMA((3 * layers + 1,)),
+            pltpu.SemaphoreType.DMA((layers + 2,)),
+        ],
+        compiler_params=params,
         name="forward",
-    )(place, event_bin, observed, both, tap_weight, tap_bias, res_weight, skip_weight)
+    )(
+        place,
+        both,
+        stay(tap_weight),
+        stay(tap_bias),
+        stay(res_weight),
+        stay(skip_weight),
+    )
 
     pool = lax.all_to_all(pool, "blk", 0, 0, tiled=True)
 
+    head_b1 = head_b1.reshape(1, -1)
+    head_second_bias = head_second_bias.reshape(1, -1)
     nll, grads = pl.pallas_call(
         lambda *refs: backward_kernel(blocks, chunk, *refs),
         out_shape=(
             shape((1, 2), F32),
             shape((chans, blocks, chunk, part), BF16),
         ),
-        in_specs=[smem] + [vmem] * 11,
+        in_specs=[smem, vmem] + [hbm] * 5 + [vmem] * 4,
         out_specs=(vmem, vmem),
-        scratch_shapes=[pltpu.VMEM((width + 8, 128), F32)],
-        compiler_params=pltpu.CompilerParams(vmem_limit_bytes=32 << 20),
+        scratch_shapes=[
+            pltpu.VMEM((layers, 2, rows, width), F32),
+            pltpu.VMEM((rows, width), F32),
+            pltpu.VMEM(tap_weight.shape, BF16),
+            pltpu.VMEM(res_weight.shape, BF16),
+            pltpu.VMEM(skip_weight.shape, BF16),
+            pltpu.VMEM((width + 8, 128), F32),
+            pltpu.SemaphoreType.DMA((1 + 4 * layers,)),
+        ],
+        compiler_params=params,
         name="backward",
     )(
         place,
         pool,
-        filters,
-        gates,
-        skip_sum,
-        tap_weight,
-        res_weight,
-        skip_weight,
+        stay(acts),
+        stay(skip_sum),
+        stay(tap_weight),
+        stay(res_weight),
+        stay(skip_weight),
         head_w1,
-        head_b1.reshape(1, -1),
+        head_b1,
         head_w2,
-        head_second_bias.reshape(1, -1),
+        head_second_bias,
     )
     grads = lax.all_to_all(
         grads.reshape(peers, chunk, part), ("chan", "blk"), 0, 0, tiled=True

time: 103 us -> 99.3 us (0.964)
  local copies, waits for them, and re-layouts: 15 us -> 1.55 us
  Pallas kernels: 6.68 us -> 19 us
  other arithmetic: 1.71 us -> 0 us
    unnamed x40 -> x10, local copies, waits for them, and re-layouts: 14.9 us -> 0.8 us
    pallas_call x0 -> x1, Pallas kernels: none -> 9.06 us  [local(): pl.pallas_call(join_kernel, out_shape=shape((peers, 2, chunk, part), BF16...]
    pallas_call x1, Pallas kernels: 2.15 us -> 4.79 us  [local(): pl.pallas_call(lambda *refs: forward_kernel(blocks, chunk, *refs), out_sh...]
    concatenate x1 -> x0, other arithmetic: 1.71 us -> none  [local(): jnp.concatenate([signal.reshape(peers, chunk, part), skip_in.reshape(peer...]
where the time goes in v2:
time: 99.3 us; the launch traced here: 98.9 us
  waiting for transfers between devices  33 us (33%)
  starting transfers between devices  23.4 us (24%)
  blocking collectives  20.5 us (21%)
  Pallas kernels  19 us (19%)
  local copies, waits for them, and re-layouts  1.55 us (2%)
  between operations  1.37 us (1%)
    all_to_all x1, waiting for transfers between devices, local(): both = lax.all_to_all(both, ('chan', 'blk'), 0, 0, tiled=True)  24.8 us
    all_to_all x1, blocking collectives, local(): lax.all_to_all(grads.reshape(peers, chunk, part), ('chan', 'blk'), 0, 0,...  20.5 us
    all_to_all x1, starting transfers between devices, local(): both = lax.all_to_all(both, ('chan', 'blk'), 0, 0, tiled=True)  19.8 us
    pallas_call x1, Pallas kernels, local(): pl.pallas_call(join_kernel, out_shape=shape((peers, 2, chunk, part), BF16...  9.06 us
    all_to_all x1, waiting for transfers between devices, local(): pool = lax.all_to_all(pool, 'blk', 0, 0, tiled=True)  8.21 us
    pallas_call x1, Pallas kernels, local(): pl.pallas_call(lambda *refs: backward_kernel(blocks, chunk, *refs), out_s...  5.19 us
    pallas_call x1, Pallas kernels, local(): pl.pallas_call(lambda *refs: forward_kernel(blocks, chunk, *refs), out_sh...  4.79 us
    all_to_all x1, starting transfers between devices, local(): pool = lax.all_to_all(pool, 'blk', 0, 0, tiled=True)  3.6 us
  transfers between devices with their start and end apart: 2, of which 2 were waited for; matrix products, arithmetic and copies ran while one was open for 1% of the time, Pallas kernels for 0%

profile of v2, /device:TPU:32, one launch (start us, length us, event | category | flops | bytes accessed | tf_op | source)
XLA Modules:
  0.0 98.9 jit_solution(15745997637073453369)
XLA Ops:
  0.6 9.1 %join.1 = bf16[32,2,16,128]{3,2,1,0:T(8,128)(2,1)} custom-call(bf16[32,16,128]{2,1,0:T(8,128)(2,1)} %bitcast.15, bf16[32,16,128]{2,1,0:T(8,128)(2,1)} %bitcast.16), custom_call_target="tpu_custom_call" | custom-call | tf_op jit(solution)/shard_map/join/pallas_call | solution.py:368
  9.7 0.0 copy-start.3
  9.7 0.0 copy-start
  9.7 0.0 copy-start.1
  9.7 0.0 copy-start.2
  9.7 19.8 %all-to-all-start = ((bf16[32,2,16,128]{3,2,1,0:T(8,128)(2,1)}), bf16[32,2,16,128]{3,2,1,0:T(8,128)(2,1)S(1)}, u32[]{:S(2)}, u32[]{:S(2)}) async-start(bf16[32,2,16,128]{3,2,1,0:T(8,128)(2,1)} %join.1), calls=%async_computation | async-start | bytes 524288 | tf_op jit(solution)/shard_map/all_to_all | solution.py:377
  30.2 0.8 concatenate.3.refs_0_
  31.0 24.8 %all-to-all-done.refs_1_ = bf16[32,2,16,128]{3,2,1,0:T(8,128)(2,1)S(1)} async-done(((bf16[32,2,16,128]{3,2,1,0:T(8,128)(2,1)}), bf16[32,2,16,128]{3,2,1,0:T(8,128)(2,1)S(1)}, u32[]{:S(2)}, u32[]{:S(2)}) %all-to-all-start) | async-done | bytes 262176 | tf_op jit(solution)/shard_map/all_to_all | solution.py:377
  55.8 4.8 %forward.1 = (f32[4,2,256,256]{3,2,1,0:T(8,128)}, f32[256,256]{1,0:T(8,128)}, bf16[16,24,256]{2,1,0:T(8,128)(2,1)}) custom-call(s32[13]{0:T(128)S(1)} %concatenate.3.refs_0_, bf16[32,2,16,128]{3,2,1,0:T(8,128)(2,1)S(1)} %all-to-all-done.refs_1_, bf16[4,2,256,512]{3,2,1,0:T(8,128)(2,1)} %refs_4_.3, f32[4,512]{1,0:T(4,128)} %refs_3_.1, ...), custom_call_target="tpu_custom_call" | custom-call | tf_op jit(solution)/shard_map/forward/pallas_call | solution.py:379
  60.6 3.6 %all-to-all-start.1 = ((bf16[16,24,256]{2,1,0:T(8,128)(2,1)}), bf16[16,24,256]{2,1,0:T(8,128)(2,1)S(1)}, u32[]{:S(2)}, u32[]{:S(2)}) async-start(bf16[16,24,256]{2,1,0:T(8,128)(2,1)} %get-tuple-element.7), calls=%async_computation.1 | async-start | bytes 393216 | tf_op jit(solution)/shard_map/all_to_all | solution.py:410
  64.2 0.0 copy-done.3
  64.2 0.1 copy.15.refs_9_
  64.3 8.2 %all-to-all-done.1.refs_1_ = bf16[16,24,256]{2,1,0:T(8,128)(2,1)S(1)} async-done(((bf16[16,24,256]{2,1,0:T(8,128)(2,1)}), bf16[16,24,256]{2,1,0:T(8,128)(2,1)S(1)}, u32[]{:S(2)}, u32[]{:S(2)}) %all-to-all-start.1) | async-done | bytes 196640 | tf_op jit(solution)/shard_map/all_to_all | solution.py:410
  72.5 0.0 copy-done
  72.5 0.0 copy-done.1
  72.5 0.0 copy-done.2
  72.5 5.2 %backward.1 = (f32[1,2]{1,0:T(1,128)}, bf16[2,16,16,128]{3,2,1,0:T(8,128)(2,1)S(1)}) custom-call(s32[13]{0:T(128)S(1)} %concatenate.3.refs_0_, bf16[16,24,256]{2,1,0:T(8,128)(2,1)S(1)} %all-to-all-done.1.refs_1_, f32[4,2,256,256]{3,2,1,0:T(8,128)} %get-tuple-element.8.refs_2_, f32[256,256]{1,0:T(8,128)} %get-tuple-element.9.refs_3_, ...), custom_call_target="tpu_custom_call" | custom-call | tf_op jit(solution)/shard_map/backward/pallas_call | solution.py:414
  77.7 20.5 %all_to_all.15 = bf16[32,16,128]{2,1,0:T(8,128)(2,1)S(1)} all-to-all(bf16[32,16,128]{2,1,0:T(8,128)(2,1)S(1)} %bitcast.11), channel_id=1, replica_groups=mesh['blk'=16,'j'=16,'chan'=2] {'chan','blk'}, dimensions={0} | all-to-all | bytes 262144 | tf_op jit(solution)/shard_map/all_to_all | solution.py:446
  98.3 0.7 copy.18
Async XLA Ops:
  9.7 54.5 %copy-start.3 = (f32[256,12]{0,1:T(8,128)S(1)}, f32[256,12]{0,1:T(8,128)}, u32[]{:S(2)}) copy-start(f32[256,12]{0,1:T(8,128)} %param.21) | copy-start | bytes 36868
  9.7 62.8 %copy-start = (f32[256,256]{1,0:T(8,128)S(1)}, f32[256,256]{1,0:T(8,128)}, u32[]{:S(2)}) copy-start(f32[256,256]{1,0:T(8,128)} %refs_7_.1) | copy-start | bytes 786436
  9.7 62.8 %copy-start.1 = (f32[256]{0:T(256)S(1)}, f32[256]{0:T(256)}, u32[]{:S(2)}) copy-start(f32[256]{0:T(256)} %param.20) | copy-start | bytes 3076
  9.7 62.8 %copy-start.2 = (f32[12]{0:T(128)S(1)}, f32[12]{0:T(128)}, u32[]{:S(2)}) copy-start(f32[12]{0:T(128)} %param.22) | copy-start | bytes 148
  9.7 46.0 %all-to-all-start = ((bf16[32,2,16,128]{3,2,1,0:T(8,128)(2,1)}), bf16[32,2,16,128]{3,2,1,0:T(8,128)(2,1)S(1)}, u32[]{:S(2)}, u32[]{:S(2)}) async-start(bf16[32,2,16,128]{3,2,1,0:T(8,128)(2,1)} %join.1), calls=%async_computation | async-start | bytes 524288 | tf_op jit(solution)/shard_map/all_to_all | solution.py:377
  60.6 11.9 %all-to-all-start.1 = ((bf16[16,24,256]{2,1,0:T(8,128)(2,1)}), bf16[16,24,256]{2,1,0:T(8,128)(2,1)S(1)}, u32[]{:S(2)}, u32[]{:S(2)}) async-start(bf16[16,24,256]{2,1,0:T(8,128)(2,1)} %get-tuple-element.7), calls=%async_computation.1 | async-start | bytes 393216 | tf_op jit(solution)/shard_map/all_to_all | solution.py:410

commit v3 on v2

--- a/solution.py
+++ b/solution.py
@@ -27,6 +27,14 @@
     return 0.5 * jnp.tanh(0.5 * v) + 0.5
 
 
+def position(blocks, chunk, chans):
+    chan_at = lax.axis_index("chan")
+    block_at = lax.axis_index("blk")
+    shard_base = lax.axis_index("j") * (blocks * chans * chunk)
+    base = shard_base + (chan_at * blocks + block_at) * chunk
+    return base, chan_at, block_at, shard_base
+
+
 def row_keep(limit, base, blocks, chunk, width):
     rows = lax.broadcasted_iota(jnp.int32, (blocks * chunk, width), 0)
     position = (rows // chunk) * FIRST_DILATION + rows % chunk + base
@@ -55,19 +63,20 @@
 def forward_kernel(
     blocks,
     chunk,
-    place_ref,
+    limit_hbm,
+    bin_hbm,
+    seen_hbm,
     both_ref,
-    tap_hbm,
-    bias_hbm,
-    res_hbm,
-    skipw_hbm,
-    act_hbm,
-    skip_hbm,
-    pool_hbm,
     tap_ref,
     bias_ref,
     res_ref,
     skipw_ref,
+    act_hbm,
+    skip_hbm,
+    pool_hbm,
+    limit_ref,
+    bin_ref,
+    seen_ref,
     act_ref,
     skip_ref,
     pool_ref,
@@ -78,23 +87,14 @@
     part = both_ref.shape[3]
     width = 2 * part
     rows = blocks * chunk
-    limit, base, chan_at = place_ref[0], place_ref[1], place_ref[2]
-    taps = [
-        pltpu.make_async_copy(tap_hbm.at[k], tap_ref.at[k], in_sems.at[k]) for k in range(layers)
+    base, chan_at, _, _ = position(blocks, chunk, 2)
+    scalars = [
+        pltpu.make_async_copy(limit_hbm, limit_ref, in_sems.at[0]),
+        pltpu.make_async_copy(bin_hbm, bin_ref, in_sems.at[1]),
+        pltpu.make_async_copy(seen_hbm, seen_ref, in_sems.at[2]),
     ]
-    skips = [
-        pltpu.make_async_copy(skipw_hbm.at[k], skipw_ref.at[k], in_sems.at[layers + k])
-        for k in range(layers)
-    ]
-    ress = [
-        pltpu.make_async_copy(res_hbm.at[k], res_ref.at[k], in_sems.at[2 * layers + k])
-        for k in range(layers - 1)
-    ]
-    bias_copy = pltpu.make_async_copy(bias_hbm, bias_ref, in_sems.at[3 * layers])
+    start_all(scalars)
     outs = []
-    start_all([taps[0], bias_copy, ress[0], skips[0]])
-    for k in range(1, layers):
-        start_all([taps[k]] + ress[k : k + 1] + [skips[k]])
     current = jnp.concatenate(
         [
             both_ref[:blocks, 0].reshape(rows, part),
@@ -109,9 +109,7 @@
         ],
         axis=1,
     ).astype(F32)
-    bias_copy.wait()
     for layer in range(layers):
-        taps[layer].wait()
         late = chunk * 2**layer
         delayed = jnp.concatenate(
             [jnp.zeros((late, width), BF16), current[: rows - late]], axis=0
@@ -130,20 +128,20 @@
         )
         outs[-1].start()
         gated = (filters * gates).astype(BF16)
-        skips[layer].wait()
         if layer < layers - 1:
-            ress[layer].wait()
             current = (current.astype(F32) + dot(gated, res_ref[layer])).astype(BF16)
         skip_sum = skip_sum + dot(gated, skipw_ref[layer])
     skip_ref[...] = skip_sum
     outs.append(pltpu.make_async_copy(skip_ref, skip_hbm, out_sems.at[layers]))
     outs[-1].start()
+    wait_all(scalars)
+    limit = limit_ref[0]
     keep = row_keep(limit, base, blocks, chunk, width)
     active = jnp.where(keep, skip_sum * sigmoid(skip_sum), 0.0)
     sums = active.reshape(blocks, chunk, width).sum(axis=1)
-    first = 5 + 2 * chan_at
+    first = 2 * chan_at
     line = lax.broadcasted_iota(jnp.int32, (8, width), 0)
-    bins = [place_ref[first + i].astype(F32) for i in (0, 1, 4, 5)]
+    bins = [ref[first + i].astype(F32) for ref in (bin_ref, seen_ref) for i in (0, 1)]
     extra = jnp.where(
         line == 0,
         bins[0],
@@ -198,24 +196,23 @@
 def backward_kernel(
     blocks,
     chunk,
-    place_ref,
+    limit_hbm,
     pool_ref,
     act_hbm,
     skip_hbm,
-    tap_hbm,
-    res_hbm,
-    skipw_hbm,
-    head1_ref,
+    tap_ref,
+    res_ref,
+    skipw_ref,
+    head1_hbm,
     headb1_ref,
     head2_ref,
     headb2_ref,
     nll_ref,
     grad_ref,
+    limit_ref,
     act_ref,
     skip_ref,
-    tap_ref,
-    res_ref,
-    skipw_ref,
+    head1_ref,
     pad_ref,
     sems,
 ):
@@ -223,27 +220,21 @@
     width = skip_ref.shape[1]
     skip_copy = pltpu.make_async_copy(skip_hbm, skip_ref, sems.at[0])
 
-    def loads(k):
-        copies = [
-            pltpu.make_async_copy(skipw_hbm.at[k], skipw_ref.at[k], sems.at[1 + 4 * k]),
-            pltpu.make_async_copy(act_hbm.at[k], act_ref.at[k], sems.at[2 + 4 * k]),
-            pltpu.make_async_copy(tap_hbm.at[k], tap_ref.at[k], sems.at[3 + 4 * k]),
-        ]
-        if k < layers - 1:
-            copies.append(
-                pltpu.make_async_copy(res_hbm.at[k], res_ref.at[k], sems.at[4 + 4 * k])
-            )
-        return copies
-
-    layer_copies = [loads(k) for k in range(layers)]
+    act_copies = [
+        pltpu.make_async_copy(act_hbm.at[k], act_ref.at[k], sems.at[1 + k]) for k in range(layers)
+    ]
+    head_copy = pltpu.make_async_copy(head1_hbm, head1_ref, sems.at[1 + layers])
+    limit_copy = pltpu.make_async_copy(limit_hbm, limit_ref, sems.at[2 + layers])
+    limit_copy.start()
+    head_copy.start()
     skip_copy.start()
     for k in range(layers - 1, -1, -1):
-        start_all(layer_copies[k])
+        act_copies[k].start()
     part = width // 2
     rows = blocks * chunk
     lanes = pad_ref.shape[1]
     outs = head2_ref.shape[1]
-    limit, base, chan_at, block_at, shard_base = (place_ref[i] for i in range(5))
+    base, chan_at, block_at, shard_base = position(blocks, chunk, 2)
     half = blocks // 2
     received = pool_ref[...].astype(F32)
     sums = jnp.concatenate(
@@ -267,12 +258,15 @@
         + shard_base
         + (2 * chan_at + window // blocks) * WLEN
     )
+    limit_copy.wait()
+    limit = limit_ref[0]
     count = jnp.clip(limit - start, 1, WLEN).astype(F32)
     pooled = sums / count
     pad_ref[...] = jnp.zeros_like(pad_ref)
     pad_ref[:width, :outs] = head2_ref[...]
     pad_ref[width : width + 1, :outs] = headb2_ref[...]
     head2 = pad_ref[:width, :]
+    head_copy.wait()
     inner = (
         jnp.dot(pooled, head1_ref[...], preferred_element_type=F32, precision=EXACT)
         + headb1_ref[...]
@@ -304,7 +298,7 @@
     grad_rows = None
     for layer in range(layers - 1, -1, -1):
         early = chunk * 2**layer
-        wait_all(layer_copies[layer])
+        act_copies[layer].wait()
         grad_gated = dot_t(grad_skip, skipw_ref[layer])
         if grad_rows is not None:
             grad_gated = grad_gated + dot_t(grad_rows, res_ref[layer])
@@ -348,16 +342,8 @@
     chunk = shard_rows // peers
     rows = blocks * chunk
     layers = tap_weight.shape[0]
-    block_at = lax.axis_index("blk")
-    chan_at = lax.axis_index("chan")
-    shard_base = lax.axis_index("j") * shard_rows
-    base = shard_base + (chan_at * blocks + block_at) * chunk
-    here = jnp.stack([base, chan_at, block_at, shard_base]).astype(jnp.int32)
-    place = jnp.concatenate([valid_len, here, event_bin, observed])
-
     shape = jax.ShapeDtypeStruct
     vmem = pl.BlockSpec(memory_space=pltpu.VMEM)
-    smem = pl.BlockSpec(memory_space=pltpu.SMEM)
     hbm = pl.BlockSpec(memory_space=pltpu.HBM)
     params = pltpu.CompilerParams(vmem_limit_bytes=24 << 20)
 
@@ -369,9 +355,12 @@
         join_kernel,
         out_shape=shape((peers, 2, chunk, part), BF16),
         in_specs=[hbm, hbm],
-        out_specs=hbm,
+        out_specs=vmem,
         scratch_shapes=[pltpu.SemaphoreType.DMA((2,))],
         compiler_params=params,
+        cost_estimate=pl.CostEstimate(
+            flops=40_000_000_000, bytes_accessed=2 * peers * chunk * part * 4, transcendentals=0
+        ),
         name="join",
     )(stay(signal.reshape(peers, chunk, part)), stay(skip_in.reshape(peers, chunk, part)))
     both = lax.all_to_all(both, ("chan", "blk"), 0, 0, tiled=True)
@@ -383,28 +372,32 @@
             pltpu.HBM((rows, width), F32),
             pltpu.HBM((blocks, blocks + 8, width), BF16),
         ),
-        in_specs=[smem, vmem] + [hbm] * 4,
+        in_specs=[hbm] * 3 + [vmem] * 5,
         out_specs=(hbm,) * 3,
         scratch_shapes=[
-            pltpu.VMEM(tap_weight.shape, BF16),
-            pltpu.VMEM(tap_bias.shape, F32),
-            pltpu.VMEM(res_weight.shape, BF16),
-            pltpu.VMEM(skip_weight.shape, BF16),
+            pltpu.SMEM(valid_len.shape, jnp.int32),
+            pltpu.SMEM(event_bin.shape, jnp.int32),
+            pltpu.SMEM(observed.shape, jnp.int32),
             pltpu.VMEM((layers, 2, rows, width), F32),
             pltpu.VMEM((rows, width), F32),
             pltpu.VMEM((blocks, blocks + 8, width), BF16),
-            pltpu.SemaphoreType.DMA((3 * layers + 1,)),
+            pltpu.SemaphoreType.DMA((3,)),
             pltpu.SemaphoreType.DMA((layers + 2,)),
         ],
         compiler_params=params,
+        cost_estimate=pl.CostEstimate(
+            flops=40_000_000_000, bytes_accessed=8 << 20, transcendentals=0
+        ),
         name="forward",
     )(
-        place,
+        valid_len,
+        stay(event_bin),
+        stay(observed),
         both,
-        stay(tap_weight),
-        stay(tap_bias),
-        stay(res_weight),
-        stay(skip_weight),
+        tap_weight,
+        tap_bias,
+        res_weight,
+        skip_weight,
     )
 
     pool = lax.all_to_all(pool, "blk", 0, 0, tiled=True)
@@ -417,28 +410,27 @@
             shape((1, 2), F32),
             shape((chans, blocks, chunk, part), BF16),
         ),
-        in_specs=[smem, vmem] + [hbm] * 5 + [vmem] * 4,
+        in_specs=[hbm, vmem] + [hbm] * 2 + [vmem] * 3 + [hbm] + [vmem] * 3,
         out_specs=(vmem, vmem),
         scratch_shapes=[
+            pltpu.SMEM(valid_len.shape, jnp.int32),
             pltpu.VMEM((layers, 2, rows, width), F32),
             pltpu.VMEM((rows, width), F32),
-            pltpu.VMEM(tap_weight.shape, BF16),
-            pltpu.VMEM(res_weight.shape, BF16),
-            pltpu.VMEM(skip_weight.shape, BF16),
+            pltpu.VMEM(head_w1.shape, F32),
             pltpu.VMEM((width + 8, 128), F32),
-            pltpu.SemaphoreType.DMA((1 + 4 * layers,)),
+            pltpu.SemaphoreType.DMA((3 + layers,)),
         ],
         compiler_params=params,
         name="backward",
     )(
-        place,
+        valid_len,
         pool,
         stay(acts),
         stay(skip_sum),
-        stay(tap_weight),
-        stay(res_weight),
-        stay(skip_weight),
-        head_w1,
+        tap_weight,
+        res_weight,
+        skip_weight,
+        stay(head_w1),
         head_b1,
         head_w2,
         head_second_bias,

time: 99.3 us -> 90.5 us (0.911)
  Pallas kernels: 19 us -> 10.4 us
    pallas_call x1, Pallas kernels: 9.06 us -> 1.84 us  [local(): pl.pallas_call(join_kernel, out_shape=shape((peers, 2, chunk, part), BF16...]
    pallas_call x1, Pallas kernels: 4.79 us -> 3 us  [local(): pl.pallas_call(lambda *refs: forward_kernel(blocks, chunk, *refs), out_sh...]
  transfers between devices with their start and end apart: 2 -> 2, of which waited for: 2 -> 2; matrix products, arithmetic and copies ran while one was open for 1% -> 0% of each run, Pallas kernels for 0% -> 0%
where the time goes in v3:
time: 90.5 us; the launch traced here: 90.1 us
  waiting for transfers between devices  33.7 us (37%)
  starting transfers between devices  23.3 us (26%)
  blocking collectives  20.5 us (23%)
  Pallas kernels  10.4 us (11%)
  between operations  1.4 us (2%)
    all_to_all x1, waiting for transfers between devices, local(): both = lax.all_to_all(both, ('chan', 'blk'), 0, 0, tiled=True)  25.5 us
    all_to_all x1, blocking collectives, local(): lax.all_to_all(grads.reshape(peers, chunk, part), ('chan', 'blk'), 0, 0,...  20.5 us
    all_to_all x1, starting transfers between devices, local(): both = lax.all_to_all(both, ('chan', 'blk'), 0, 0, tiled=True)  19.7 us
    all_to_all x1, waiting for transfers between devices, local(): pool = lax.all_to_all(pool, 'blk', 0, 0, tiled=True)  8.21 us
    pallas_call x1, Pallas kernels, local(): pl.pallas_call(lambda *refs: backward_kernel(blocks, chunk, *refs), out_s...  5.55 us
    all_to_all x1, starting transfers between devices, local(): pool = lax.all_to_all(pool, 'blk', 0, 0, tiled=True)  3.58 us
    pallas_call x1, Pallas kernels, local(): pl.pallas_call(lambda *refs: forward_kernel(blocks, chunk, *refs), out_sh...  3 us
    pallas_call x1, Pallas kernels, local(): pl.pallas_call(join_kernel, out_shape=shape((peers, 2, chunk, part), BF16...  1.84 us
  transfers between devices with their start and end apart: 2, of which 2 were waited for; matrix products, arithmetic and copies ran while one was open for 0% of the time, Pallas kernels for 0%

profile of v3, /device:TPU:32, one launch (start us, length us, event | category | flops | bytes accessed | tf_op | source)
XLA Modules:
  0.0 90.1 jit_solution(14600889153735685711)
XLA Ops:
  0.6 0.0 copy-start
  0.6 0.0 copy-start.1
  0.7 0.0 copy-start.2
  0.7 0.0 copy-start.5
  0.7 1.8 %join.1 = bf16[32,2,16,128]{3,2,1,0:T(8,128)(2,1)} custom-call(bf16[32,16,128]{2,1,0:T(8,128)(2,1)} %bitcast.11, bf16[32,16,128]{2,1,0:T(8,128)(2,1)} %bitcast.12), custom_call_target="tpu_custom_call" | custom-call | flops 40000000000 | bytes 524288 | tf_op jit(solution)/shard_map/join/pallas_call | solution.py:354
  2.5 19.7 %all-to-all-start = ((bf16[32,2,16,128]{3,2,1,0:T(8,128)(2,1)}), bf16[32,2,16,128]{3,2,1,0:T(8,128)(2,1)S(1)}, u32[]{:S(2)}, u32[]{:S(2)}) async-start(bf16[32,2,16,128]{3,2,1,0:T(8,128)(2,1)} %join.1), calls=%async_computation | async-start | bytes 524288 | tf_op jit(solution)/shard_map/all_to_all | solution.py:366
  22.9 0.0 copy-start.6
  22.9 0.0 copy-start.3
  22.9 0.0 copy-start.4
  22.9 25.5 %all-to-all-done.refs_3_ = bf16[32,2,16,128]{3,2,1,0:T(8,128)(2,1)S(1)} async-done(((bf16[32,2,16,128]{3,2,1,0:T(8,128)(2,1)}), bf16[32,2,16,128]{3,2,1,0:T(8,128)(2,1)S(1)}, u32[]{:S(2)}, u32[]{:S(2)}) %all-to-all-start) | async-done | bytes 262176 | tf_op jit(solution)/shard_map/all_to_all | solution.py:366
  48.4 0.0 copy-done
  48.4 0.0 copy-done.1
  48.4 0.0 copy-done.2
  48.4 0.0 copy-done.5
  48.4 3.0 %forward.1 = (f32[4,2,256,256]{3,2,1,0:T(8,128)}, f32[256,256]{1,0:T(8,128)}, bf16[16,24,256]{2,1,0:T(8,128)(2,1)}) custom-call(s32[1]{0:T(128)S(6)} %copy.17.refs_0_, s32[4]{0:T(128)} %refs_1_.1, s32[4]{0:T(128)} %refs_2_.1, bf16[32,2,16,128]{3,2,1,0:T(8,128)(2,1)S(1)} %all-to-all-done.refs_3_, bf16[4,2,256,512]{3,2,1,0:T(8,128)(2,1)S(1)} %copy-done, ...), custom_call_target="tpu_custom_call" | custom-call | flops 40000000000 | bytes 8388608 | tf_op jit(solution)/shard_map/forward/pallas_call | solution.py:368
  51.4 3.6 %all-to-all-start.1 = ((bf16[16,24,256]{2,1,0:T(8,128)(2,1)}), bf16[16,24,256]{2,1,0:T(8,128)(2,1)S(1)}, u32[]{:S(2)}, u32[]{:S(2)}) async-start(bf16[16,24,256]{2,1,0:T(8,128)(2,1)} %get-tuple-element.7), calls=%async_computation.1 | async-start | bytes 393216 | tf_op jit(solution)/shard_map/all_to_all | solution.py:403
  55.0 0.0 copy-done.6
  55.0 0.1 copy.15.refs_9_
  55.1 8.2 %all-to-all-done.1.refs_1_ = bf16[16,24,256]{2,1,0:T(8,128)(2,1)S(1)} async-done(((bf16[16,24,256]{2,1,0:T(8,128)(2,1)}), bf16[16,24,256]{2,1,0:T(8,128)(2,1)S(1)}, u32[]{:S(2)}, u32[]{:S(2)}) %all-to-all-start.1) | async-done | bytes 196640 | tf_op jit(solution)/shard_map/all_to_all | solution.py:403
  63.3 0.0 copy-done.3
  63.4 0.0 copy-done.4
  63.4 5.5 %backward.1 = (f32[1,2]{1,0:T(1,128)}, bf16[2,16,16,128]{3,2,1,0:T(8,128)(2,1)S(1)}) custom-call(s32[1]{0:T(128)S(6)} %copy.17.refs_0_, bf16[16,24,256]{2,1,0:T(8,128)(2,1)S(1)} %all-to-all-done.1.refs_1_, f32[4,2,256,256]{3,2,1,0:T(8,128)} %get-tuple-element.8.refs_2_, f32[256,256]{1,0:T(8,128)} %get-tuple-element.9.refs_3_, ...), custom_call_target="tpu_custom_call" | custom-call | tf_op jit(solution)/shard_map/backward/pallas_call | solution.py:407
  68.9 20.5 %all_to_all.15 = bf16[32,16,128]{2,1,0:T(8,128)(2,1)S(1)} all-to-all(bf16[32,16,128]{2,1,0:T(8,128)(2,1)S(1)} %bitcast.7), channel_id=1, replica_groups=mesh['blk'=16,'j'=16,'chan'=2] {'chan','blk'}, dimensions={0} | all-to-all | bytes 262144 | tf_op jit(solution)/shard_map/all_to_all | solution.py:438
  89.5 0.7 copy.18
Async XLA Ops:
  0.6 47.8 %copy-start = (bf16[4,2,256,512]{3,2,1,0:T(8,128)(2,1)S(1)}, bf16[4,2,256,512]{3,2,1,0:T(8,128)(2,1)}, u32[]{:S(2)}) copy-start(bf16[4,2,256,512]{3,2,1,0:T(8,128)(2,1)} %refs_4_.3) | copy-start | bytes 6291460
  0.6 47.8 %copy-start.1 = (bf16[4,256,256]{2,1,0:T(8,128)(2,1)S(1)}, bf16[4,256,256]{2,1,0:T(8,128)(2,1)}, u32[]{:S(2)}) copy-start(bf16[4,256,256]{2,1,0:T(8,128)(2,1)} %refs_6_.3) | copy-start | bytes 1572868
  0.7 47.7 %copy-start.2 = (bf16[3,256,256]{2,1,0:T(8,128)(2,1)S(1)}, bf16[3,256,256]{2,1,0:T(8,128)(2,1)}, u32[]{:S(2)}) copy-start(bf16[3,256,256]{2,1,0:T(8,128)(2,1)} %refs_5_.3) | copy-start | bytes 1179652
  0.7 47.7 %copy-start.5 = (f32[4,512]{1,0:T(4,128)S(1)}, f32[4,512]{1,0:T(4,128)}, u32[]{:S(2)}) copy-start(f32[4,512]{1,0:T(4,128)} %refs_5_.2) | copy-start | bytes 24580
  2.5 45.9 %all-to-all-start = ((bf16[32,2,16,128]{3,2,1,0:T(8,128)(2,1)}), bf16[32,2,16,128]{3,2,1,0:T(8,128)(2,1)S(1)}, u32[]{:S(2)}, u32[]{:S(2)}) async-start(bf16[32,2,16,128]{3,2,1,0:T(8,128)(2,1)} %join.1), calls=%async_computation | async-start | bytes 524288 | tf_op jit(solution)/shard_map/all_to_all | solution.py:366
  22.9 32.2 %copy-start.6 = (f32[256,12]{0,1:T(8,128)S(1)}, f32[256,12]{0,1:T(8,128)}, u32[]{:S(2)}) copy-start(f32[256,12]{0,1:T(8,128)} %param.21) | copy-start | bytes 36868
  22.9 40.5 %copy-start.3 = (f32[256]{0:T(256)S(1)}, f32[256]{0:T(256)}, u32[]{:S(2)}) copy-start(f32[256]{0:T(256)} %param.20) | copy-start | bytes 3076
  22.9 40.5 %copy-start.4 = (f32[12]{0:T(128)S(1)}, f32[12]{0:T(128)}, u32[]{:S(2)}) copy-start(f32[12]{0:T(128)} %param.22) | copy-start | bytes 148
  51.4 11.9 %all-to-all-start.1 = ((bf16[16,24,256]{2,1,0:T(8,128)(2,1)}), bf16[16,24,256]{2,1,0:T(8,128)(2,1)S(1)}, u32[]{:S(2)}, u32[]{:S(2)}) async-start(bf16[16,24,256]{2,1,0:T(8,128)(2,1)} %get-tuple-element.7), calls=%async_computation.1 | async-start | bytes 393216 | tf_op jit(solution)/shard_map/all_to_all | solution.py:403

commit v4 on v3

--- a/solution.py
+++ b/solution.py
@@ -10,6 +10,7 @@
 FIRST_DILATION = 8192
 F32 = jnp.float32
 BF16 = jnp.bfloat16
+FIRST = 26
 EXACT = lax.Precision.HIGHEST
 
 
@@ -51,13 +52,52 @@
         copy.wait()
 
 
+def turn(peers):
+    lead = peers - FIRST
+    return [(FIRST, 0, lead), (0, lead, FIRST)]
+
+
 def join_kernel(signal_ref, skip_ref, both_ref, sems):
-    copies = [
-        pltpu.make_async_copy(signal_ref, both_ref.at[:, 0], sems.at[0]),
-        pltpu.make_async_copy(skip_ref, both_ref.at[:, 1], sems.at[1]),
-    ]
+    copies = []
+    for source, target, size in turn(both_ref.shape[0]):
+        for part, ref in enumerate((signal_ref, skip_ref)):
+            copies.append(
+                pltpu.make_async_copy(
+                    ref.at[pl.ds(source, size)],
+                    both_ref.at[pl.ds(target, size), part],
+                    sems.at[len(copies)],
+                )
+            )
     start_all(copies)
     wait_all(copies)
+
+
+def place_kernel(received_ref, grad_hbm, sems):
+    copies = []
+    for target, source, size in turn(received_ref.shape[0]):
+        copies.append(
+            pltpu.make_async_copy(
+                received_ref.at[pl.ds(source, size)],
+                grad_hbm.at[pl.ds(target, size)],
+                sems.at[len(copies)],
+            )
+        )
+    start_all(copies)
+    wait_all(copies)
+
+
+def spans(start, size, total):
+    start = (start - FIRST) % total
+    head = min(size, total - start)
+    return [(start, head)] + ([(0, size - head)] if head < size else [])
+
+
+def read_turned(ref, start, size, part):
+    pieces = [
+        ref[at : at + count, part].reshape(count * ref.shape[2], ref.shape[3])
+        for at, count in spans(start, size, ref.shape[0])
+    ]
+    return pieces[0] if len(pieces) == 1 else jnp.concatenate(pieces, axis=0)
 
 
 def forward_kernel(
@@ -95,20 +135,13 @@
     ]
     start_all(scalars)
     outs = []
-    current = jnp.concatenate(
-        [
-            both_ref[:blocks, 0].reshape(rows, part),
-            both_ref[blocks:, 0].reshape(rows, part),
-        ],
-        axis=1,
-    )
-    skip_sum = jnp.concatenate(
-        [
-            both_ref[:blocks, 1].reshape(rows, part),
-            both_ref[blocks:, 1].reshape(rows, part),
-        ],
-        axis=1,
-    ).astype(F32)
+    current, skip_sum = (
+        jnp.concatenate(
+            [read_turned(both_ref, c * blocks, blocks, part_at) for c in range(2)], axis=1
+        )
+        for part_at in range(2)
+    )
+    skip_sum = skip_sum.astype(F32)
     for layer in range(layers):
         late = chunk * 2**layer
         delayed = jnp.concatenate(
@@ -237,6 +270,8 @@
     base, chan_at, block_at, shard_base = position(blocks, chunk, 2)
     half = blocks // 2
     received = pool_ref[...].astype(F32)
+    first = FIRST % blocks
+    received = jnp.concatenate([received[blocks - first :], received[: blocks - first]], axis=0)
     sums = jnp.concatenate(
         [
             received[:half, :blocks, :].sum(axis=0),
@@ -315,8 +350,13 @@
         if grad_rows is not None:
             summed = summed + grad_rows.astype(F32)
         grad_rows = summed.astype(BF16)
-    grad_ref[0] = grad_rows[:, :part].reshape(blocks, chunk, part)
-    grad_ref[1] = grad_rows[:, part:].reshape(blocks, chunk, part)
+    peers = grad_ref.shape[0]
+    for c in range(2):
+        done = 0
+        for at, count in spans(c * blocks, blocks, peers):
+            piece = grad_rows[done * chunk : (done + count) * chunk, c * part : (c + 1) * part]
+            grad_ref[at : at + count] = piece.reshape(count, chunk, part)
+            done += count
 
 
 def local(
@@ -356,14 +396,22 @@
         out_shape=shape((peers, 2, chunk, part), BF16),
         in_specs=[hbm, hbm],
         out_specs=vmem,
-        scratch_shapes=[pltpu.SemaphoreType.DMA((2,))],
+        scratch_shapes=[pltpu.SemaphoreType.DMA((4,))],
         compiler_params=params,
         cost_estimate=pl.CostEstimate(
             flops=40_000_000_000, bytes_accessed=2 * peers * chunk * part * 4, transcendentals=0
         ),
         name="join",
     )(stay(signal.reshape(peers, chunk, part)), stay(skip_in.reshape(peers, chunk, part)))
-    both = lax.all_to_all(both, ("chan", "blk"), 0, 0, tiled=True)
+    shards = lax.axis_size("j")
+    everyone = ("blk", "j", "chan")
+    order = [(FIRST + i) % peers for i in range(peers)]
+    wide = [
+        [((k % blocks) * shards + j) * chans + k // blocks for k in order] for j in range(shards)
+    ]
+    first = FIRST % blocks
+    near = [[(first + i) % blocks for i in range(blocks)]]
+    both = lax.all_to_all(both, everyone, 0, 0, tiled=True, axis_index_groups=wide)
 
     acts, skip_sum, pool = pl.pallas_call(
         lambda *refs: forward_kernel(blocks, chunk, *refs),
@@ -400,7 +448,7 @@
         skip_weight,
     )
 
-    pool = lax.all_to_all(pool, "blk", 0, 0, tiled=True)
+    pool = lax.all_to_all(pool, "blk", 0, 0, tiled=True, axis_index_groups=near)
 
     head_b1 = head_b1.reshape(1, -1)
     head_second_bias = head_second_bias.reshape(1, -1)
@@ -408,7 +456,7 @@
         lambda *refs: backward_kernel(blocks, chunk, *refs),
         out_shape=(
             shape((1, 2), F32),
-            shape((chans, blocks, chunk, part), BF16),
+            shape((peers, chunk, part), BF16),
         ),
         in_specs=[hbm, vmem] + [hbm] * 2 + [vmem] * 3 + [hbm] + [vmem] * 3,
         out_specs=(vmem, vmem),
@@ -435,9 +483,16 @@
         head_w2,
         head_second_bias,
     )
-    grads = lax.all_to_all(
-        grads.reshape(peers, chunk, part), ("chan", "blk"), 0, 0, tiled=True
-    )
+    grads = lax.all_to_all(grads, everyone, 0, 0, tiled=True, axis_index_groups=wide)
+    grads = pl.pallas_call(
+        place_kernel,
+        out_shape=pltpu.HBM((peers, chunk, part), BF16),
+        in_specs=[vmem],
+        out_specs=hbm,
+        scratch_shapes=[pltpu.SemaphoreType.DMA((2,))],
+        compiler_params=params,
+        name="place",
+    )(grads)
     return (nll.reshape(2), grads.reshape(shard_rows, part))
 
 

time: 90.5 us -> 78.6 us (0.87)
  waiting for transfers between devices: 33.7 us -> 15 us
  starting transfers between devices: 23.3 us -> 30.1 us
    all_to_all x2, waiting for transfers between devices: 33.7 us -> 15 us  [the longest x1 11.8 us: local(): lax.all_to_all(both, everyone, 0, 0, tiled=True, axis_index_groups=wide)]
    all_to_all x2, starting transfers between devices: 23.3 us -> 30.1 us  [the longest x1 21.6 us: local(): lax.all_to_all(both, everyone, 0, 0, tiled=True, axis_index_groups=wide)]
where the time goes in v4:
time: 78.6 us; the launch traced here: 78.3 us
  starting transfers between devices  30.1 us (38%)
  blocking collectives  20.5 us (26%)
  waiting for transfers between devices  15 us (19%)
  Pallas kernels  11.1 us (14%)
  between operations  1.38 us (2%)
    all_to_all x1, starting transfers between devices, local(): lax.all_to_all(both, everyone, 0, 0, tiled=True, axis_index_groups=wide)  21.6 us
    all_to_all x1, blocking collectives, local(): lax.all_to_all(grads, everyone, 0, 0, tiled=True, axis_index_groups=wide)  20.5 us
    all_to_all x1, waiting for transfers between devices, local(): lax.all_to_all(both, everyone, 0, 0, tiled=True, axis_index_groups=wide)  11.8 us
    all_to_all x1, starting transfers between devices, local(): pool = lax.all_to_all(pool, 'blk', 0, 0, tiled=True, axis_index_groups=near)  8.57 us
    pallas_call x1, Pallas kernels, local(): pl.pallas_call(lambda *refs: backward_kernel(blocks, chunk, *refs), out_s...  5.55 us
    all_to_all x1, waiting for transfers between devices, local(): pool = lax.all_to_all(pool, 'blk', 0, 0, tiled=True, axis_index_groups=near)  3.22 us
    pallas_call x1, Pallas kernels, local(): pl.pallas_call(lambda *refs: forward_kernel(blocks, chunk, *refs), out_sh...  2.98 us
    pallas_call x1, Pallas kernels, local(): pl.pallas_call(join_kernel, out_shape=shape((peers, 2, chunk, part), BF16...  1.87 us
  transfers between devices with their start and end apart: 2, of which 2 were waited for; matrix products, arithmetic and copies ran while one was open for 0% of the time, Pallas kernels for 0%

profile of v4, /device:TPU:32, one launch (start us, length us, event | category | flops | bytes accessed | tf_op | source)
XLA Modules:
  0.0 78.3 jit_solution(17711142422059252568)
XLA Ops:
  0.6 0.0 copy-start
  0.6 0.0 copy-start.1
  0.7 0.0 copy-start.2
  0.7 0.0 copy-start.5
  0.7 1.9 %join.1 = bf16[32,2,16,128]{3,2,1,0:T(8,128)(2,1)} custom-call(bf16[32,16,128]{2,1,0:T(8,128)(2,1)} %bitcast.9, bf16[32,16,128]{2,1,0:T(8,128)(2,1)} %bitcast.10), custom_call_target="tpu_custom_call" | custom-call | flops 40000000000 | bytes 524288 | tf_op jit(solution)/shard_map/join/pallas_call | solution.py:394
  2.5 21.6 %all-to-all-start = ((bf16[32,2,16,128]{3,2,1,0:T(8,128)(2,1)}), bf16[32,2,16,128]{3,2,1,0:T(8,128)(2,1)S(1)}, u32[]{:S(2)}, u32[]{:S(2)}) async-start(bf16[32,2,16,128]{3,2,1,0:T(8,128)(2,1)} %join.1), calls=%async_computation | async-start | bytes 524288 | tf_op jit(solution)/shard_map/all_to_all | solution.py:414
  24.8 0.0 copy-start.6
  24.8 0.0 copy-start.3
  24.8 0.0 copy-start.4
  24.8 11.8 %all-to-all-done.refs_3_ = bf16[32,2,16,128]{3,2,1,0:T(8,128)(2,1)S(1)} async-done(((bf16[32,2,16,128]{3,2,1,0:T(8,128)(2,1)}), bf16[32,2,16,128]{3,2,1,0:T(8,128)(2,1)S(1)}, u32[]{:S(2)}, u32[]{:S(2)}) %all-to-all-start) | async-done | bytes 262176 | tf_op jit(solution)/shard_map/all_to_all | solution.py:414
  36.6 0.0 copy-done
  36.6 0.0 copy-done.1
  36.6 0.0 copy-done.2
  36.6 0.0 copy-done.5
  36.6 3.0 %forward.1 = (f32[4,2,256,256]{3,2,1,0:T(8,128)}, f32[256,256]{1,0:T(8,128)}, bf16[16,24,256]{2,1,0:T(8,128)(2,1)}) custom-call(s32[1]{0:T(128)S(6)} %copy.16.refs_0_, s32[4]{0:T(128)} %refs_1_.1, s32[4]{0:T(128)} %refs_2_.1, bf16[32,2,16,128]{3,2,1,0:T(8,128)(2,1)S(1)} %all-to-all-done.refs_3_, bf16[4,2,256,512]{3,2,1,0:T(8,128)(2,1)S(1)} %copy-done, ...), custom_call_target="tpu_custom_call" | custom-call | flops 40000000000 | bytes 8388608 | tf_op jit(solution)/shard_map/forward/pallas_call | solution.py:416
  39.6 8.6 %all-to-all-start.1 = ((bf16[16,24,256]{2,1,0:T(8,128)(2,1)}), bf16[16,24,256]{2,1,0:T(8,128)(2,1)S(1)}, u32[]{:S(2)}, u32[]{:S(2)}) async-start(bf16[16,24,256]{2,1,0:T(8,128)(2,1)} %get-tuple-element.7), calls=%async_computation.1 | async-start | bytes 393216 | tf_op jit(solution)/shard_map/all_to_all | solution.py:451
  48.2 0.0 copy-done.6
  48.2 0.1 copy.15.refs_9_
  48.3 3.2 %all-to-all-done.1.refs_1_ = bf16[16,24,256]{2,1,0:T(8,128)(2,1)S(1)} async-done(((bf16[16,24,256]{2,1,0:T(8,128)(2,1)}), bf16[16,24,256]{2,1,0:T(8,128)(2,1)S(1)}, u32[]{:S(2)}, u32[]{:S(2)}) %all-to-all-start.1) | async-done | bytes 196640 | tf_op jit(solution)/shard_map/all_to_all | solution.py:451
  51.5 0.0 copy-done.3
  51.5 0.0 copy-done.4
  51.5 5.5 %backward.1 = (f32[1,2]{1,0:T(1,128)}, bf16[32,16,128]{2,1,0:T(8,128)(2,1)S(1)}) custom-call(s32[1]{0:T(128)S(6)} %copy.16.refs_0_, bf16[16,24,256]{2,1,0:T(8,128)(2,1)S(1)} %all-to-all-done.1.refs_1_, f32[4,2,256,256]{3,2,1,0:T(8,128)} %get-tuple-element.8.refs_2_, f32[256,256]{1,0:T(8,128)} %get-tuple-element.9.refs_3_, ...), custom_call_target="tpu_custom_call" | custom-call | tf_op jit(solution)/shard_map/backward/pallas_call | solution.py:455
  57.1 20.5 %all_to_all.15.received_ref = bf16[32,16,128]{2,1,0:T(8,128)(2,1)S(1)} all-to-all(bf16[32,16,128]{2,1,0:T(8,128)(2,1)S(1)} %get-tuple-element.11), channel_id=1, replica_groups={{321,353,385,417,449,481,0,32,64,96,128,160,192,224,256,288,320,352,384..., dimensions={0} | all-to-all | bytes 262144 | tf_op jit(solution)/shard_map/all_to_all | solution.py:486
  77.6 0.7 place.1
Async XLA Ops:
  0.6 35.9 %copy-start = (bf16[4,2,256,512]{3,2,1,0:T(8,128)(2,1)S(1)}, bf16[4,2,256,512]{3,2,1,0:T(8,128)(2,1)}, u32[]{:S(2)}) copy-start(bf16[4,2,256,512]{3,2,1,0:T(8,128)(2,1)} %refs_4_.3) | copy-start | bytes 6291460
  0.6 35.9 %copy-start.1 = (bf16[4,256,256]{2,1,0:T(8,128)(2,1)S(1)}, bf16[4,256,256]{2,1,0:T(8,128)(2,1)}, u32[]{:S(2)}) copy-start(bf16[4,256,256]{2,1,0:T(8,128)(2,1)} %refs_6_.3) | copy-start | bytes 1572868
  0.7 35.9 %copy-start.2 = (bf16[3,256,256]{2,1,0:T(8,128)(2,1)S(1)}, bf16[3,256,256]{2,1,0:T(8,128)(2,1)}, u32[]{:S(2)}) copy-start(bf16[3,256,256]{2,1,0:T(8,128)(2,1)} %refs_5_.3) | copy-start | bytes 1179652
  0.7 35.9 %copy-start.5 = (f32[4,512]{1,0:T(4,128)S(1)}, f32[4,512]{1,0:T(4,128)}, u32[]{:S(2)}) copy-start(f32[4,512]{1,0:T(4,128)} %refs_5_.2) | copy-start | bytes 24580
  2.5 34.0 %all-to-all-start = ((bf16[32,2,16,128]{3,2,1,0:T(8,128)(2,1)}), bf16[32,2,16,128]{3,2,1,0:T(8,128)(2,1)S(1)}, u32[]{:S(2)}, u32[]{:S(2)}) async-start(bf16[32,2,16,128]{3,2,1,0:T(8,128)(2,1)} %join.1), calls=%async_computation | async-start | bytes 524288 | tf_op jit(solution)/shard_map/all_to_all | solution.py:414
  24.8 23.4 %copy-start.6 = (f32[256,12]{0,1:T(8,128)S(1)}, f32[256,12]{0,1:T(8,128)}, u32[]{:S(2)}) copy-start(f32[256,12]{0,1:T(8,128)} %param.21) | copy-start | bytes 36868
  24.8 26.7 %copy-start.3 = (f32[256]{0:T(256)S(1)}, f32[256]{0:T(256)}, u32[]{:S(2)}) copy-start(f32[256]{0:T(256)} %param.20) | copy-start | bytes 3076
  24.8 26.7 %copy-start.4 = (f32[12]{0:T(128)S(1)}, f32[12]{0:T(128)}, u32[]{:S(2)}) copy-start(f32[12]{0:T(128)} %param.22) | copy-start | bytes 148
  39.6 11.9 %all-to-all-start.1 = ((bf16[16,24,256]{2,1,0:T(8,128)(2,1)}), bf16[16,24,256]{2,1,0:T(8,128)(2,1)S(1)}, u32[]{:S(2)}, u32[]{:S(2)}) async-start(bf16[16,24,256]{2,1,0:T(8,128)(2,1)} %get-tuple-element.7), calls=%async_computation.1 | async-start | bytes 393216 | tf_op jit(solution)/shard_map/all_to_all | solution.py:451

commit v5 on v4

--- a/solution.py
+++ b/solution.py
@@ -11,17 +11,26 @@
 F32 = jnp.float32
 BF16 = jnp.bfloat16
 FIRST = 26
-EXACT = lax.Precision.HIGHEST
 
 
 def dot(a, b):
     return jnp.dot(a, b, preferred_element_type=F32)
 
 
-def dot_t(a, b, precision=None):
-    return lax.dot_general(
-        a, b, (((1,), (1,)), ((), ())), preferred_element_type=F32, precision=precision
-    )
+def dot_t(a, b):
+    return lax.dot_general(a, b, (((1,), (1,)), ((), ())), preferred_element_type=F32)
+
+
+def split(v):
+    high = v.astype(BF16)
+    return high, (v - high.astype(F32)).astype(BF16)
+
+
+def fine_dot(a, b, product):
+    high, low = split(a)
+    rows = a.shape[0]
+    both = product(jnp.concatenate([high, low], axis=0), b[0])
+    return both[:rows] + both[rows:] + product(high, b[1])
 
 
 def sigmoid(v):
@@ -57,7 +66,10 @@
     return [(FIRST, 0, lead), (0, lead, FIRST)]
 
 
-def join_kernel(signal_ref, skip_ref, both_ref, sems):
+def join_kernel(limit_ref, signal_ref, skip_ref, both_ref, limit_hbm, hold_ref, sems):
+    hold_ref[0] = limit_ref[0]
+    hand = pltpu.make_async_copy(hold_ref, limit_hbm, sems.at[4])
+    hand.start()
     copies = []
     for source, target, size in turn(both_ref.shape[0]):
         for part, ref in enumerate((signal_ref, skip_ref)):
@@ -69,7 +81,7 @@
                 )
             )
     start_all(copies)
-    wait_all(copies)
+    wait_all(copies + [hand])
 
 
 def place_kernel(received_ref, grad_hbm, sems):
@@ -110,16 +122,16 @@
     tap_ref,
     bias_ref,
     res_ref,
-    skipw_ref,
+    skipw_hbm,
     act_hbm,
-    skip_hbm,
-    pool_hbm,
+    slope_hbm,
+    pool_ref,
     limit_ref,
     bin_ref,
     seen_ref,
+    skipw_ref,
     act_ref,
-    skip_ref,
-    pool_ref,
+    slope_ref,
     in_sems,
     out_sems,
 ):
@@ -133,8 +145,11 @@
         pltpu.make_async_copy(bin_hbm, bin_ref, in_sems.at[1]),
         pltpu.make_async_copy(seen_hbm, seen_ref, in_sems.at[2]),
     ]
+    skipw_copy = pltpu.make_async_copy(skipw_hbm, skipw_ref, in_sems.at[3])
+    skipw_copy.start()
     start_all(scalars)
     outs = []
+    gated_all = []
     current, skip_sum = (
         jnp.concatenate(
             [read_turned(both_ref, c * blocks, blocks, part_at) for c in range(2)], axis=1
@@ -154,23 +169,31 @@
         )
         filters = jnp.tanh(preact[:, :width])
         gates = sigmoid(preact[:, width:])
-        act_ref[layer, 0] = filters
-        act_ref[layer, 1] = gates
+        product = filters * gates
+        gated = product.astype(BF16)
+        gated_all.append(gated)
+        if layer < layers - 1:
+            current = (current.astype(F32) + dot(gated, res_ref[layer])).astype(BF16)
+        act_ref[layer, :, :width] = (gates - product * filters).astype(BF16)
+        act_ref[layer, :, width:] = (product - product * gates).astype(BF16)
         outs.append(
             pltpu.make_async_copy(act_ref.at[layer], act_hbm.at[layer], out_sems.at[layer])
         )
         outs[-1].start()
-        gated = (filters * gates).astype(BF16)
-        if layer < layers - 1:
-            current = (current.astype(F32) + dot(gated, res_ref[layer])).astype(BF16)
-        skip_sum = skip_sum + dot(gated, skipw_ref[layer])
-    skip_ref[...] = skip_sum
-    outs.append(pltpu.make_async_copy(skip_ref, skip_hbm, out_sems.at[layers]))
-    outs[-1].start()
+        if layer == 1:
+            skipw_copy.wait()
+        if layer > 0:
+            skip_sum = skip_sum + dot(gated_all[layer - 1], skipw_ref[layer - 1])
+    skip_sum = skip_sum + dot(gated_all[layers - 1], skipw_ref[layers - 1])
     wait_all(scalars)
     limit = limit_ref[0]
     keep = row_keep(limit, base, blocks, chunk, width)
-    active = jnp.where(keep, skip_sum * sigmoid(skip_sum), 0.0)
+    sig = sigmoid(skip_sum)
+    slope = sig * (1.0 + skip_sum * (1.0 - sig))
+    slope_ref[...] = jnp.where(keep, slope, 0.0).astype(BF16)
+    outs.append(pltpu.make_async_copy(slope_ref, slope_hbm, out_sems.at[layers]))
+    outs[-1].start()
+    active = jnp.where(keep, skip_sum * sig, 0.0)
     sums = active.reshape(blocks, chunk, width).sum(axis=1)
     first = 2 * chan_at
     line = lax.broadcasted_iota(jnp.int32, (8, width), 0)
@@ -185,8 +208,6 @@
     for other in range(blocks):
         pool_ref[other, :blocks, :] = sums
         pool_ref[other, blocks:, :] = extra
-    outs.append(pltpu.make_async_copy(pool_ref, pool_hbm, out_sems.at[layers + 1]))
-    outs[-1].start()
     wait_all(outs)
 
 
@@ -232,11 +253,11 @@
     limit_hbm,
     pool_ref,
     act_hbm,
-    skip_hbm,
+    slope_hbm,
+    skipw_hbm,
     tap_ref,
     res_ref,
-    skipw_ref,
-    head1_hbm,
+    head1_ref,
     headb1_ref,
     head2_ref,
     headb2_ref,
@@ -244,29 +265,26 @@
     grad_ref,
     limit_ref,
     act_ref,
-    skip_ref,
-    head1_ref,
+    slope_ref,
+    skipw_ref,
     pad_ref,
+    bias2_ref,
     sems,
 ):
     layers = tap_ref.shape[0]
-    width = skip_ref.shape[1]
-    skip_copy = pltpu.make_async_copy(skip_hbm, skip_ref, sems.at[0])
-
-    act_copies = [
-        pltpu.make_async_copy(act_hbm.at[k], act_ref.at[k], sems.at[1 + k]) for k in range(layers)
+    width = slope_ref.shape[1]
+    limit_copy = pltpu.make_async_copy(limit_hbm, limit_ref, sems.at[0])
+    copies = [
+        pltpu.make_async_copy(slope_hbm, slope_ref, sems.at[1]),
+        pltpu.make_async_copy(skipw_hbm, skipw_ref, sems.at[2]),
+        pltpu.make_async_copy(act_hbm, act_ref, sems.at[3]),
     ]
-    head_copy = pltpu.make_async_copy(head1_hbm, head1_ref, sems.at[1 + layers])
-    limit_copy = pltpu.make_async_copy(limit_hbm, limit_ref, sems.at[2 + layers])
     limit_copy.start()
-    head_copy.start()
-    skip_copy.start()
-    for k in range(layers - 1, -1, -1):
-        act_copies[k].start()
+    start_all(copies)
     part = width // 2
     rows = blocks * chunk
-    lanes = pad_ref.shape[1]
-    outs = head2_ref.shape[1]
+    lanes = pad_ref.shape[0]
+    outs = head2_ref.shape[0]
     base, chan_at, block_at, shard_base = position(blocks, chunk, 2)
     half = blocks // 2
     received = pool_ref[...].astype(F32)
@@ -298,24 +316,19 @@
     count = jnp.clip(limit - start, 1, WLEN).astype(F32)
     pooled = sums / count
     pad_ref[...] = jnp.zeros_like(pad_ref)
-    pad_ref[:width, :outs] = head2_ref[...]
-    pad_ref[width : width + 1, :outs] = headb2_ref[...]
-    head2 = pad_ref[:width, :]
-    head_copy.wait()
-    inner = (
-        jnp.dot(pooled, head1_ref[...], preferred_element_type=F32, precision=EXACT)
-        + headb1_ref[...]
-    )
+    pad_ref[:outs, :] = head2_ref[...]
+    head1 = split(head1_ref[...])
+    head2 = split(pad_ref[...])
+    bias2_ref[...] = jnp.zeros_like(bias2_ref)
+    bias2_ref[:, :outs] = headb2_ref[...]
+    inner = fine_dot(pooled, head1, dot) + headb1_ref[...]
     open_inner = sigmoid(inner)
     hidden = inner * open_inner
-    params = (
-        jnp.dot(hidden, head2, preferred_element_type=F32, precision=EXACT)
-        + pad_ref[width : width + 1, :]
-    )
+    params = fine_dot(hidden, head2, dot_t) + bias2_ref[...]
     nll, to_params = mixture(params, log_time, seen, outs // 3)
-    to_hidden = dot_t(to_params, head2, EXACT)
+    to_hidden = fine_dot(to_params, head2, dot)
     to_inner = to_hidden * open_inner * (1.0 + inner * (1.0 - open_inner))
-    to_pooled = dot_t(to_inner, head1_ref[...], EXACT)
+    to_pooled = fine_dot(to_inner, head1, dot_t)
 
     row = lax.broadcasted_iota(jnp.int32, (2 * blocks, 2), 0)
     col = lax.broadcasted_iota(jnp.int32, (2 * blocks, 2), 1)
@@ -324,25 +337,16 @@
 
     own_pool = jnp.where(block_at < half, to_pooled[:blocks], to_pooled[blocks:])
     spread = jnp.broadcast_to(own_pool[:, None, :], (blocks, chunk, width)).reshape(rows, width)
-    keep = row_keep(limit, base, blocks, chunk, width)
-    skip_copy.wait()
-    skip_sum = skip_ref[...]
-    sig = sigmoid(skip_sum)
-    slope = sig * (1.0 + skip_sum * (1.0 - sig))
-    grad_skip = jnp.where(keep, spread * slope, 0.0).astype(BF16)
+    wait_all(copies)
+    grad_skip = (spread * slope_ref[...].astype(F32)).astype(BF16)
     grad_rows = None
     for layer in range(layers - 1, -1, -1):
         early = chunk * 2**layer
-        act_copies[layer].wait()
         grad_gated = dot_t(grad_skip, skipw_ref[layer])
         if grad_rows is not None:
             grad_gated = grad_gated + dot_t(grad_rows, res_ref[layer])
-        filters = act_ref[layer, 0]
-        gates = act_ref[layer, 1]
-        through = grad_gated * gates
-        to_filter = (through * (1.0 - filters * filters)).astype(BF16)
-        to_gate = (through * filters * (1.0 - gates)).astype(BF16)
-        preact_grad = jnp.concatenate([to_filter, to_gate], axis=1)
+        twice = jnp.concatenate([grad_gated, grad_gated], axis=1)
+        preact_grad = (twice * act_ref[layer].astype(F32)).astype(BF16)
         ahead = jnp.concatenate(
             [preact_grad[early:], jnp.zeros((early, 2 * width), BF16)], axis=0
         )
@@ -383,6 +387,7 @@
     rows = blocks * chunk
     layers = tap_weight.shape[0]
     shape = jax.ShapeDtypeStruct
+    smem = pl.BlockSpec(memory_space=pltpu.SMEM)
     vmem = pl.BlockSpec(memory_space=pltpu.VMEM)
     hbm = pl.BlockSpec(memory_space=pltpu.HBM)
     params = pltpu.CompilerParams(vmem_limit_bytes=24 << 20)
@@ -391,18 +396,18 @@
         return pltpu.with_memory_space_constraint(array, pltpu.HBM)
 
 
-    both = pl.pallas_call(
+    both, limit = pl.pallas_call(
         join_kernel,
-        out_shape=shape((peers, 2, chunk, part), BF16),
-        in_specs=[hbm, hbm],
-        out_specs=vmem,
-        scratch_shapes=[pltpu.SemaphoreType.DMA((4,))],
+        out_shape=(shape((peers, 2, chunk, part), BF16), pltpu.HBM((8,), jnp.int32)),
+        in_specs=[smem, hbm, hbm],
+        out_specs=(vmem, hbm),
+        scratch_shapes=[pltpu.SMEM((8,), jnp.int32), pltpu.SemaphoreType.DMA((5,))],
         compiler_params=params,
         cost_estimate=pl.CostEstimate(
             flops=40_000_000_000, bytes_accessed=2 * peers * chunk * part * 4, transcendentals=0
         ),
         name="join",
-    )(stay(signal.reshape(peers, chunk, part)), stay(skip_in.reshape(peers, chunk, part)))
+    )(valid_len, stay(signal.reshape(peers, chunk, part)), stay(skip_in.reshape(peers, chunk, part)))
     shards = lax.axis_size("j")
     everyone = ("blk", "j", "chan")
     order = [(FIRST + i) % peers for i in range(peers)]
@@ -413,24 +418,24 @@
     near = [[(first + i) % blocks for i in range(blocks)]]
     both = lax.all_to_all(both, everyone, 0, 0, tiled=True, axis_index_groups=wide)
 
-    acts, skip_sum, pool = pl.pallas_call(
+    acts, slope, pool = pl.pallas_call(
         lambda *refs: forward_kernel(blocks, chunk, *refs),
         out_shape=(
-            pltpu.HBM((layers, 2, rows, width), F32),
-            pltpu.HBM((rows, width), F32),
-            pltpu.HBM((blocks, blocks + 8, width), BF16),
+            pltpu.HBM((layers, rows, 2 * width), BF16),
+            pltpu.HBM((rows, width), BF16),
+            shape((blocks, blocks + 8, width), BF16),
         ),
-        in_specs=[hbm] * 3 + [vmem] * 5,
-        out_specs=(hbm,) * 3,
+        in_specs=[hbm] * 3 + [vmem] * 4 + [hbm],
+        out_specs=(hbm, hbm, vmem),
         scratch_shapes=[
-            pltpu.SMEM(valid_len.shape, jnp.int32),
+            pltpu.SMEM((8,), jnp.int32),
             pltpu.SMEM(event_bin.shape, jnp.int32),
             pltpu.SMEM(observed.shape, jnp.int32),
-            pltpu.VMEM((layers, 2, rows, width), F32),
-            pltpu.VMEM((rows, width), F32),
-            pltpu.VMEM((blocks, blocks + 8, width), BF16),
-            pltpu.SemaphoreType.DMA((3,)),
-            pltpu.SemaphoreType.DMA((layers + 2,)),
+            pltpu.VMEM(skip_weight.shape, BF16),
+            pltpu.VMEM((layers, rows, 2 * width), BF16),
+            pltpu.VMEM((rows, width), BF16),
+            pltpu.SemaphoreType.DMA((4,)),
+            pltpu.SemaphoreType.DMA((layers + 1,)),
         ],
         compiler_params=params,
         cost_estimate=pl.CostEstimate(
@@ -438,14 +443,14 @@
         ),
         name="forward",
     )(
-        valid_len,
+        stay(limit),
         stay(event_bin),
         stay(observed),
         both,
         tap_weight,
         tap_bias,
         res_weight,
-        skip_weight,
+        stay(skip_weight),
     )
 
     pool = lax.all_to_all(pool, "blk", 0, 0, tiled=True, axis_index_groups=near)
@@ -458,29 +463,30 @@
             shape((1, 2), F32),
             shape((peers, chunk, part), BF16),
         ),
-        in_specs=[hbm, vmem] + [hbm] * 2 + [vmem] * 3 + [hbm] + [vmem] * 3,
+        in_specs=[hbm, vmem] + [hbm] * 3 + [vmem] * 6,
         out_specs=(vmem, vmem),
         scratch_shapes=[
-            pltpu.SMEM(valid_len.shape, jnp.int32),
-            pltpu.VMEM((layers, 2, rows, width), F32),
-            pltpu.VMEM((rows, width), F32),
-            pltpu.VMEM(head_w1.shape, F32),
-            pltpu.VMEM((width + 8, 128), F32),
-            pltpu.SemaphoreType.DMA((3 + layers,)),
+            pltpu.SMEM((8,), jnp.int32),
+            pltpu.VMEM((layers, rows, 2 * width), BF16),
+            pltpu.VMEM((rows, width), BF16),
+            pltpu.VMEM(skip_weight.shape, BF16),
+            pltpu.VMEM((128, width), F32),
+            pltpu.VMEM((1, 128), F32),
+            pltpu.SemaphoreType.DMA((4,)),
         ],
         compiler_params=params,
         name="backward",
     )(
-        valid_len,
+        stay(limit),
         pool,
         stay(acts),
-        stay(skip_sum),
+        stay(slope),
+        stay(skip_weight),
         tap_weight,
         res_weight,
-        skip_weight,
-        stay(head_w1),
+        head_w1,
         head_b1,
-        head_w2,
+        head_w2.T,
         head_second_bias,
     )
     grads = lax.all_to_all(grads, everyone, 0, 0, tiled=True, axis_index_groups=wide)

time: 78.6 us -> 75.4 us (0.959)
  blocking collectives: 20.5 us -> 65 us
  starting transfers between devices: 30.1 us -> 0 us
  waiting for transfers between devices: 15 us -> 0 us
  Pallas kernels: 11.1 us -> 8.63 us
    all_to_all x0 -> x2, blocking collectives: none -> 44.5 us  [the longest x1 33.2 us: local(): lax.all_to_all(both, everyone, 0, 0, tiled=True, axis_index_groups=wide)]
    all_to_all x2 -> x0, starting transfers between devices: 30.1 us -> none  [the longest x1 21.6 us: local(): lax.all_to_all(both, everyone, 0, 0, tiled=True, axis_index_groups=wide)]
    all_to_all x2 -> x0, waiting for transfers between devices: 15 us -> none  [the longest x1 11.8 us: local(): lax.all_to_all(both, everyone, 0, 0, tiled=True, axis_index_groups=wide)]
    pallas_call x1, Pallas kernels: 5.55 us -> 3.79 us  [local(): pl.pallas_call(lambda *refs: backward_kernel(blocks, chunk, *refs), out_s...]
  transfers between devices with their start and end apart: 2 -> 0, of which waited for: 2 -> 0; matrix products, arithmetic and copies ran while one was open for 0% -> 0% of each run, Pallas kernels for 0% -> 0%
where the time goes in v5:
time: 75.4 us; the launch traced here: 75.1 us
  blocking collectives  65 us (86%)
  Pallas kernels  8.63 us (11%)
  between operations  1.37 us (2%)
    all_to_all x1, blocking collectives, local(): lax.all_to_all(both, everyone, 0, 0, tiled=True, axis_index_groups=wide)  33.2 us
    all_to_all x1, blocking collectives, local(): lax.all_to_all(grads, everyone, 0, 0, tiled=True, axis_index_groups=wide)  20.5 us
    all_to_all x1, blocking collectives, local(): pool = lax.all_to_all(pool, 'blk', 0, 0, tiled=True, axis_index_groups=near)  11.3 us
    pallas_call x1, Pallas kernels, local(): pl.pallas_call(lambda *refs: backward_kernel(blocks, chunk, *refs), out_s...  3.79 us
    pallas_call x1, Pallas kernels, local(): pl.pallas_call(lambda *refs: forward_kernel(blocks, chunk, *refs), out_sh...  2.99 us

profile of v5, /device:TPU:32, one launch (start us, length us, event | category | flops | bytes accessed | tf_op | source)
XLA Modules:
  0.0 75.1 jit_solution(12017061952989383576)
XLA Ops:
  1.3 0.0 copy-start
  1.3 0.0 copy-start.1
  1.3 0.0 copy-start.6
  1.3 1.2 %join.1 = (bf16[32,2,16,128]{3,2,1,0:T(8,128)(2,1)S(1)}, s32[8]{0:T(128)}) custom-call(s32[1]{0:T(128)S(6)} %copy.15.limit_ref, bf16[32,16,128]{2,1,0:T(8,128)(2,1)} %bitcast.11, bf16[32,16,128]{2,1,0:T(8,128)(2,1)} %bitcast.12), custom_call_target="tpu_custom_call" | custom-call | flops 40000000000 | bytes 524288 | tf_op jit(solution)/shard_map/join/pallas_call | solution.py:399
  2.5 33.2 %all_to_all.15.refs_3_ = bf16[32,2,16,128]{3,2,1,0:T(8,128)(2,1)S(1)} all-to-all(bf16[32,2,16,128]{3,2,1,0:T(8,128)(2,1)S(1)} %get-tuple-element.10), channel_id=1, replica_groups={{321,353,385,417,449,481,0,32,64,96,128,160,192,224,256,288,320,352,384..., dimensions={0} | all-to-all | bytes 524288 | tf_op jit(solution)/shard_map/all_to_all | solution.py:419
  35.7 0.0 copy-done
  35.7 0.0 copy-done.1
  35.7 0.0 copy-done.6
  35.7 0.0 copy-start.2
  35.7 0.0 copy-start.3
  35.7 0.0 copy-start.4
  35.7 0.0 copy-start.5
  35.8 3.0 %forward.1 = (bf16[4,256,512]{2,1,0:T(8,128)(2,1)}, bf16[256,256]{1,0:T(8,128)(2,1)}, bf16[16,24,256]{2,1,0:T(8,128)(2,1)S(1)}) custom-call(s32[8]{0:T(128)} %get-tuple-element.9.refs_0_, s32[4]{0:T(128)} %refs_1_.1, s32[4]{0:T(128)} %refs_2_.1, bf16[32,2,16,128]{3,2,1,0:T(8,128)(2,1)S(1)} %all_to_all.15.refs_3_, bf16[4,2,256,512]{3,2,1,0:T(8,128)(2,1)S(1)} %copy-done, ...), custom_call_target="tpu_custom_call" | custom-call | flops 40000000000 | bytes 8388608 | tf_op jit(solution)/shard_map/forward/pallas_call | solution.py:421
  38.8 11.3 %all_to_all.16.refs_1_ = bf16[16,24,256]{2,1,0:T(8,128)(2,1)S(1)} all-to-all(bf16[16,24,256]{2,1,0:T(8,128)(2,1)S(1)} %get-tuple-element.11), channel_id=1, replica_groups={{320,352,384,416,448,480,0,32,64,96,128,160,192,224,256,288},{321,353,3..., dimensions={0} | all-to-all | bytes 393216 | tf_op jit(solution)/shard_map/all_to_all | solution.py:456
  50.1 0.0 copy-done.2
  50.1 0.0 copy-done.3
  50.1 0.0 copy-done.4
  50.1 0.0 copy-done.5
  50.1 3.8 %backward.1 = (f32[1,2]{1,0:T(1,128)}, bf16[32,16,128]{2,1,0:T(8,128)(2,1)S(1)}) custom-call(s32[8]{0:T(128)} %get-tuple-element.9.refs_0_, bf16[16,24,256]{2,1,0:T(8,128)(2,1)S(1)} %all_to_all.16.refs_1_, bf16[4,256,512]{2,1,0:T(8,128)(2,1)} %get-tuple-element.12.refs_2_, bf16[256,256]{1,0:T(8,128)(2,1)} %get-tuple-element.13.refs_3_, ...), custom_call_target="tpu_custom_call" | custom-call | tf_op jit(solution)/shard_map/backward/pallas_call | solution.py:460
  53.9 20.5 %all_to_all.17.received_ref = bf16[32,16,128]{2,1,0:T(8,128)(2,1)S(1)} all-to-all(bf16[32,16,128]{2,1,0:T(8,128)(2,1)S(1)} %get-tuple-element.15), channel_id=1, replica_groups={{321,353,385,417,449,481,0,32,64,96,128,160,192,224,256,288,320,352,384..., dimensions={0} | all-to-all | bytes 262144 | tf_op jit(solution)/shard_map/all_to_all | solution.py:492
  74.4 0.7 place.1
Async XLA Ops:
  1.3 34.4 %copy-start = (bf16[4,2,256,512]{3,2,1,0:T(8,128)(2,1)S(1)}, bf16[4,2,256,512]{3,2,1,0:T(8,128)(2,1)}, u32[]{:S(2)}) copy-start(bf16[4,2,256,512]{3,2,1,0:T(8,128)(2,1)} %refs_5_.3) | copy-start | bytes 6291460
  1.3 34.4 %copy-start.1 = (bf16[3,256,256]{2,1,0:T(8,128)(2,1)S(1)}, bf16[3,256,256]{2,1,0:T(8,128)(2,1)}, u32[]{:S(2)}) copy-start(bf16[3,256,256]{2,1,0:T(8,128)(2,1)} %refs_6_.3) | copy-start | bytes 1179652
  1.3 34.4 %copy-start.6 = (f32[4,512]{1,0:T(4,128)S(1)}, f32[4,512]{1,0:T(4,128)}, u32[]{:S(2)}) copy-start(f32[4,512]{1,0:T(4,128)} %refs_5_.2) | copy-start | bytes 24580
  35.7 14.4 %copy-start.2 = (f32[256,256]{1,0:T(8,128)S(1)}, f32[256,256]{1,0:T(8,128)}, u32[]{:S(2)}) copy-start(f32[256,256]{1,0:T(8,128)} %refs_7_.3) | copy-start | bytes 786436
  35.7 14.4 %copy-start.3 = (f32[256,12]{0,1:T(8,128)S(1)}, f32[256,12]{0,1:T(8,128)}, u32[]{:S(2)}) copy-start(f32[256,12]{0,1:T(8,128)} %param.21) | copy-start | bytes 36868
  35.7 14.4 %copy-start.4 = (f32[256]{0:T(256)S(1)}, f32[256]{0:T(256)}, u32[]{:S(2)}) copy-start(f32[256]{0:T(256)} %param.20) | copy-start | bytes 3076
  35.7 14.3 %copy-start.5 = (f32[12]{0:T(128)S(1)}, f32[12]{0:T(128)}, u32[]{:S(2)}) copy-start(f32[12]{0:T(128)} %param.22) | copy-start | bytes 148

commit v6 on v5

--- a/solution.py
+++ b/solution.py
@@ -124,14 +124,13 @@
     res_ref,
     skipw_hbm,
     act_hbm,
-    slope_hbm,
+    slope_ref,
     pool_ref,
     limit_ref,
     bin_ref,
     seen_ref,
     skipw_ref,
     act_ref,
-    slope_ref,
     in_sems,
     out_sems,
 ):
@@ -191,8 +190,6 @@
     sig = sigmoid(skip_sum)
     slope = sig * (1.0 + skip_sum * (1.0 - sig))
     slope_ref[...] = jnp.where(keep, slope, 0.0).astype(BF16)
-    outs.append(pltpu.make_async_copy(slope_ref, slope_hbm, out_sems.at[layers]))
-    outs[-1].start()
     active = jnp.where(keep, skip_sum * sig, 0.0)
     sums = active.reshape(blocks, chunk, width).sum(axis=1)
     first = 2 * chan_at
@@ -253,7 +250,7 @@
     limit_hbm,
     pool_ref,
     act_hbm,
-    slope_hbm,
+    slope_ref,
     skipw_hbm,
     tap_ref,
     res_ref,
@@ -265,7 +262,6 @@
     grad_ref,
     limit_ref,
     act_ref,
-    slope_ref,
     skipw_ref,
     pad_ref,
     bias2_ref,
@@ -275,9 +271,8 @@
     width = slope_ref.shape[1]
     limit_copy = pltpu.make_async_copy(limit_hbm, limit_ref, sems.at[0])
     copies = [
-        pltpu.make_async_copy(slope_hbm, slope_ref, sems.at[1]),
-        pltpu.make_async_copy(skipw_hbm, skipw_ref, sems.at[2]),
-        pltpu.make_async_copy(act_hbm, act_ref, sems.at[3]),
+        pltpu.make_async_copy(skipw_hbm, skipw_ref, sems.at[1]),
+        pltpu.make_async_copy(act_hbm, act_ref, sems.at[2]),
     ]
     limit_copy.start()
     start_all(copies)
@@ -422,20 +417,19 @@
         lambda *refs: forward_kernel(blocks, chunk, *refs),
         out_shape=(
             pltpu.HBM((layers, rows, 2 * width), BF16),
-            pltpu.HBM((rows, width), BF16),
+            shape((rows, width), BF16),
             shape((blocks, blocks + 8, width), BF16),
         ),
         in_specs=[hbm] * 3 + [vmem] * 4 + [hbm],
-        out_specs=(hbm, hbm, vmem),
+        out_specs=(hbm, vmem, vmem),
         scratch_shapes=[
             pltpu.SMEM((8,), jnp.int32),
             pltpu.SMEM(event_bin.shape, jnp.int32),
             pltpu.SMEM(observed.shape, jnp.int32),
             pltpu.VMEM(skip_weight.shape, BF16),
             pltpu.VMEM((layers, rows, 2 * width), BF16),
-            pltpu.VMEM((rows, width), BF16),
             pltpu.SemaphoreType.DMA((4,)),
-            pltpu.SemaphoreType.DMA((layers + 1,)),
+            pltpu.SemaphoreType.DMA((layers,)),
         ],
         compiler_params=params,
         cost_estimate=pl.CostEstimate(
@@ -463,16 +457,15 @@
             shape((1, 2), F32),
             shape((peers, chunk, part), BF16),
         ),
-        in_specs=[hbm, vmem] + [hbm] * 3 + [vmem] * 6,
+        in_specs=[hbm, vmem, hbm, vmem, hbm] + [vmem] * 6,
         out_specs=(vmem, vmem),
         scratch_shapes=[
             pltpu.SMEM((8,), jnp.int32),
             pltpu.VMEM((layers, rows, 2 * width), BF16),
-            pltpu.VMEM((rows, width), BF16),
             pltpu.VMEM(skip_weight.shape, BF16),
             pltpu.VMEM((128, width), F32),
             pltpu.VMEM((1, 128), F32),
-            pltpu.SemaphoreType.DMA((4,)),
+            pltpu.SemaphoreType.DMA((3,)),
         ],
         compiler_params=params,
         name="backward",
@@ -480,7 +473,7 @@
         stay(limit),
         pool,
         stay(acts),
-        stay(slope),
+        slope,
         stay(skip_weight),
         tap_weight,
         res_weight,

time: 75.4 us -> 75.1 us (level)
  no operation moved by 1% of the time
where the time goes in v6:
time: 75.1 us; the launch traced here: 74.8 us
  blocking collectives  65.1 us (87%)
  Pallas kernels  8.34 us (11%)
  between operations  1.37 us (2%)
    all_to_all x1, blocking collectives, local(): lax.all_to_all(both, everyone, 0, 0, tiled=True, axis_index_groups=wide)  33.2 us
    all_to_all x1, blocking collectives, local(): lax.all_to_all(grads, everyone, 0, 0, tiled=True, axis_index_groups=wide)  20.5 us
    all_to_all x1, blocking collectives, local(): pool = lax.all_to_all(pool, 'blk', 0, 0, tiled=True, axis_index_groups=near)  11.3 us
    pallas_call x1, Pallas kernels, local(): pl.pallas_call(lambda *refs: backward_kernel(blocks, chunk, *refs), out_s...  3.78 us
    pallas_call x1, Pallas kernels, local(): pl.pallas_call(lambda *refs: forward_kernel(blocks, chunk, *refs), out_sh...  2.71 us

profile of v6, /device:TPU:32, one launch (start us, length us, event | category | flops | bytes accessed | tf_op | source)
XLA Modules:
  0.0 74.8 jit_solution(4120887724258312299)
XLA Ops:
  1.3 0.0 copy-start
  1.3 0.0 copy-start.1
  1.3 0.0 copy-start.6
  1.3 1.2 %join.1 = (bf16[32,2,16,128]{3,2,1,0:T(8,128)(2,1)S(1)}, s32[8]{0:T(128)}) custom-call(s32[1]{0:T(128)S(6)} %copy.15.limit_ref, bf16[32,16,128]{2,1,0:T(8,128)(2,1)} %bitcast.11, bf16[32,16,128]{2,1,0:T(8,128)(2,1)} %bitcast.12), custom_call_target="tpu_custom_call" | custom-call | flops 40000000000 | bytes 524288 | tf_op jit(solution)/shard_map/join/pallas_call | solution.py:394
  2.5 33.2 %all_to_all.15.refs_3_ = bf16[32,2,16,128]{3,2,1,0:T(8,128)(2,1)S(1)} all-to-all(bf16[32,2,16,128]{3,2,1,0:T(8,128)(2,1)S(1)} %get-tuple-element.10), channel_id=1, replica_groups={{321,353,385,417,449,481,0,32,64,96,128,160,192,224,256,288,320,352,384..., dimensions={0} | all-to-all | bytes 524288 | tf_op jit(solution)/shard_map/all_to_all | solution.py:414
  35.7 0.0 copy-done
  35.7 0.0 copy-done.1
  35.7 0.0 copy-done.6
  35.7 0.0 copy-start.2
  35.7 0.0 copy-start.3
  35.7 0.0 copy-start.4
  35.7 0.0 copy-start.5
  35.8 2.7 %forward.1 = (bf16[4,256,512]{2,1,0:T(8,128)(2,1)}, bf16[256,256]{1,0:T(8,128)(2,1)S(1)}, bf16[16,24,256]{2,1,0:T(8,128)(2,1)S(1)}) custom-call(s32[8]{0:T(128)} %get-tuple-element.9.refs_0_, s32[4]{0:T(128)} %refs_1_.1, s32[4]{0:T(128)} %refs_2_.1, bf16[32,2,16,128]{3,2,1,0:T(8,128)(2,1)S(1)} %all_to_all.15.refs_3_, bf16[4,2,256,512]{3,2,1,0:T(8,128)(2,1)S(1)} %copy-done, ...), custom_call_target="tpu_custom_call" | custom-call | flops 40000000000 | bytes 8388608 | tf_op jit(solution)/shard_map/forward/pallas_call | solution.py:416
  38.5 11.3 %all_to_all.16.refs_1_ = bf16[16,24,256]{2,1,0:T(8,128)(2,1)S(1)} all-to-all(bf16[16,24,256]{2,1,0:T(8,128)(2,1)S(1)} %get-tuple-element.11), channel_id=1, replica_groups={{320,352,384,416,448,480,0,32,64,96,128,160,192,224,256,288},{321,353,3..., dimensions={0} | all-to-all | bytes 393216 | tf_op jit(solution)/shard_map/all_to_all | solution.py:450
  49.8 0.0 copy-done.2
  49.8 0.0 copy-done.3
  49.8 0.0 copy-done.4
  49.8 0.0 copy-done.5
  49.8 3.8 %backward.1 = (f32[1,2]{1,0:T(1,128)}, bf16[32,16,128]{2,1,0:T(8,128)(2,1)S(1)}) custom-call(s32[8]{0:T(128)} %get-tuple-element.9.refs_0_, bf16[16,24,256]{2,1,0:T(8,128)(2,1)S(1)} %all_to_all.16.refs_1_, bf16[4,256,512]{2,1,0:T(8,128)(2,1)} %get-tuple-element.12.refs_2_, bf16[256,256]{1,0:T(8,128)(2,1)S(1)} %get-tuple-element.13.refs_3_, ...), custom_call_target="tpu_custom_call" | custom-call | tf_op jit(solution)/shard_map/backward/pallas_call | solution.py:454
  53.6 20.5 %all_to_all.17.received_ref = bf16[32,16,128]{2,1,0:T(8,128)(2,1)S(1)} all-to-all(bf16[32,16,128]{2,1,0:T(8,128)(2,1)S(1)} %get-tuple-element.15), channel_id=1, replica_groups={{321,353,385,417,449,481,0,32,64,96,128,160,192,224,256,288,320,352,384..., dimensions={0} | all-to-all | bytes 262144 | tf_op jit(solution)/shard_map/all_to_all | solution.py:485
  74.1 0.7 place.1
Async XLA Ops:
  1.3 34.4 %copy-start = (bf16[4,2,256,512]{3,2,1,0:T(8,128)(2,1)S(1)}, bf16[4,2,256,512]{3,2,1,0:T(8,128)(2,1)}, u32[]{:S(2)}) copy-start(bf16[4,2,256,512]{3,2,1,0:T(8,128)(2,1)} %refs_5_.3) | copy-start | bytes 6291460
  1.3 34.4 %copy-start.1 = (bf16[3,256,256]{2,1,0:T(8,128)(2,1)S(1)}, bf16[3,256,256]{2,1,0:T(8,128)(2,1)}, u32[]{:S(2)}) copy-start(bf16[3,256,256]{2,1,0:T(8,128)(2,1)} %refs_6_.3) | copy-start | bytes 1179652
  1.3 34.4 %copy-start.6 = (f32[4,512]{1,0:T(4,128)S(1)}, f32[4,512]{1,0:T(4,128)}, u32[]{:S(2)}) copy-start(f32[4,512]{1,0:T(4,128)} %refs_5_.2) | copy-start | bytes 24580
  35.7 14.1 %copy-start.2 = (f32[256,256]{1,0:T(8,128)S(1)}, f32[256,256]{1,0:T(8,128)}, u32[]{:S(2)}) copy-start(f32[256,256]{1,0:T(8,128)} %refs_7_.3) | copy-start | bytes 786436
  35.7 14.1 %copy-start.3 = (f32[256,12]{0,1:T(8,128)S(1)}, f32[256,12]{0,1:T(8,128)}, u32[]{:S(2)}) copy-start(f32[256,12]{0,1:T(8,128)} %param.21) | copy-start | bytes 36868
  35.7 14.1 %copy-start.4 = (f32[256]{0:T(256)S(1)}, f32[256]{0:T(256)}, u32[]{:S(2)}) copy-start(f32[256]{0:T(256)} %param.20) | copy-start | bytes 3076
  35.7 14.1 %copy-start.5 = (f32[12]{0:T(128)S(1)}, f32[12]{0:T(128)}, u32[]{:S(2)}) copy-start(f32[12]{0:T(128)} %param.22) | copy-start | bytes 148

commit v7 on v6

--- a/solution.py
+++ b/solution.py
@@ -10,7 +10,7 @@
 FIRST_DILATION = 8192
 F32 = jnp.float32
 BF16 = jnp.bfloat16
-FIRST = 26
+FIRST = 10
 
 
 def dot(a, b):
@@ -61,55 +61,52 @@
         copy.wait()
 
 
-def turn(peers):
-    lead = peers - FIRST
+def spans(blocks):
+    lead = blocks - FIRST
     return [(FIRST, 0, lead), (0, lead, FIRST)]
 
 
 def join_kernel(limit_ref, signal_ref, skip_ref, both_ref, limit_hbm, hold_ref, sems):
     hold_ref[0] = limit_ref[0]
-    hand = pltpu.make_async_copy(hold_ref, limit_hbm, sems.at[4])
-    hand.start()
+    copies = [pltpu.make_async_copy(hold_ref, limit_hbm, sems.at[0])]
+    blocks, chans = both_ref.shape[:2]
+    for c in range(chans):
+        for block, at, count in spans(blocks):
+            for part, ref in enumerate((signal_ref, skip_ref)):
+                copies.append(
+                    pltpu.make_async_copy(
+                        ref.at[pl.ds(c * blocks + block, count)],
+                        both_ref.at[pl.ds(at, count), chans - 1 - c, part],
+                        sems.at[len(copies)],
+                    )
+                )
+    start_all(copies)
+    wait_all(copies)
+
+
+def place_kernel(received_ref, grad_hbm, sems):
     copies = []
-    for source, target, size in turn(both_ref.shape[0]):
-        for part, ref in enumerate((signal_ref, skip_ref)):
+    blocks, chans = received_ref.shape[:2]
+    for c in range(chans):
+        for block, at, count in spans(blocks):
             copies.append(
                 pltpu.make_async_copy(
-                    ref.at[pl.ds(source, size)],
-                    both_ref.at[pl.ds(target, size), part],
+                    received_ref.at[pl.ds(at, count), chans - 1 - c],
+                    grad_hbm.at[pl.ds(c * blocks + block, count)],
                     sems.at[len(copies)],
                 )
             )
     start_all(copies)
-    wait_all(copies + [hand])
-
-
-def place_kernel(received_ref, grad_hbm, sems):
-    copies = []
-    for target, source, size in turn(received_ref.shape[0]):
-        copies.append(
-            pltpu.make_async_copy(
-                received_ref.at[pl.ds(source, size)],
-                grad_hbm.at[pl.ds(target, size)],
-                sems.at[len(copies)],
-            )
-        )
-    start_all(copies)
     wait_all(copies)
 
 
-def spans(start, size, total):
-    start = (start - FIRST) % total
-    head = min(size, total - start)
-    return [(start, head)] + ([(0, size - head)] if head < size else [])
-
-
-def read_turned(ref, start, size, part):
+def read_turned(ref, c, part):
+    blocks, chans = ref.shape[:2]
     pieces = [
-        ref[at : at + count, part].reshape(count * ref.shape[2], ref.shape[3])
-        for at, count in spans(start, size, ref.shape[0])
+        ref[at : at + count, chans - 1 - c, part].reshape(count * ref.shape[3], ref.shape[4])
+        for _, at, count in sorted(spans(blocks))
     ]
-    return pieces[0] if len(pieces) == 1 else jnp.concatenate(pieces, axis=0)
+    return jnp.concatenate(pieces, axis=0)
 
 
 def forward_kernel(
@@ -135,7 +132,7 @@
     out_sems,
 ):
     layers = tap_ref.shape[0]
-    part = both_ref.shape[3]
+    part = both_ref.shape[4]
     width = 2 * part
     rows = blocks * chunk
     base, chan_at, _, _ = position(blocks, chunk, 2)
@@ -151,7 +148,7 @@
     gated_all = []
     current, skip_sum = (
         jnp.concatenate(
-            [read_turned(both_ref, c * blocks, blocks, part_at) for c in range(2)], axis=1
+            [read_turned(both_ref, c, part_at) for c in range(2)], axis=1
         )
         for part_at in range(2)
     )
@@ -283,7 +280,7 @@
     base, chan_at, block_at, shard_base = position(blocks, chunk, 2)
     half = blocks // 2
     received = pool_ref[...].astype(F32)
-    first = FIRST % blocks
+    first = FIRST
     received = jnp.concatenate([received[blocks - first :], received[: blocks - first]], axis=0)
     sums = jnp.concatenate(
         [
@@ -349,13 +346,10 @@
         if grad_rows is not None:
             summed = summed + grad_rows.astype(F32)
         grad_rows = summed.astype(BF16)
-    peers = grad_ref.shape[0]
     for c in range(2):
-        done = 0
-        for at, count in spans(c * blocks, blocks, peers):
-            piece = grad_rows[done * chunk : (done + count) * chunk, c * part : (c + 1) * part]
-            grad_ref[at : at + count] = piece.reshape(count, chunk, part)
-            done += count
+        for block, at, count in spans(blocks):
+            piece = grad_rows[block * chunk : (block + count) * chunk, c * part : (c + 1) * part]
+            grad_ref[at : at + count, 1 - c] = piece.reshape(count, chunk, part)
 
 
 def local(
@@ -393,10 +387,10 @@
 
     both, limit = pl.pallas_call(
         join_kernel,
-        out_shape=(shape((peers, 2, chunk, part), BF16), pltpu.HBM((8,), jnp.int32)),
+        out_shape=(shape((blocks, chans, 2, chunk, part), BF16), pltpu.HBM((8,), jnp.int32)),
         in_specs=[smem, hbm, hbm],
         out_specs=(vmem, hbm),
-        scratch_shapes=[pltpu.SMEM((8,), jnp.int32), pltpu.SemaphoreType.DMA((5,))],
+        scratch_shapes=[pltpu.SMEM((8,), jnp.int32), pltpu.SemaphoreType.DMA((9,))],
         compiler_params=params,
         cost_estimate=pl.CostEstimate(
             flops=40_000_000_000, bytes_accessed=2 * peers * chunk * part * 4, transcendentals=0
@@ -405,13 +399,17 @@
     )(valid_len, stay(signal.reshape(peers, chunk, part)), stay(skip_in.reshape(peers, chunk, part)))
     shards = lax.axis_size("j")
     everyone = ("blk", "j", "chan")
-    order = [(FIRST + i) % peers for i in range(peers)]
+    order = [
+        (chans - 1 - i % chans) * blocks + (FIRST + i // chans) % blocks for i in range(peers)
+    ]
     wide = [
         [((k % blocks) * shards + j) * chans + k // blocks for k in order] for j in range(shards)
     ]
-    first = FIRST % blocks
+    first = FIRST
     near = [[(first + i) % blocks for i in range(blocks)]]
+    both = both.reshape(peers, 2, chunk, part)
     both = lax.all_to_all(both, everyone, 0, 0, tiled=True, axis_index_groups=wide)
+    both = both.reshape(blocks, chans, 2, chunk, part)
 
     acts, slope, pool = pl.pallas_call(
         lambda *refs: forward_kernel(blocks, chunk, *refs),
@@ -455,7 +453,7 @@
         lambda *refs: backward_kernel(blocks, chunk, *refs),
         out_shape=(
             shape((1, 2), F32),
-            shape((peers, chunk, part), BF16),
+            shape((blocks, chans, chunk, part), BF16),
         ),
         in_specs=[hbm, vmem, hbm, vmem, hbm] + [vmem] * 6,
         out_specs=(vmem, vmem),
@@ -482,13 +480,15 @@
         head_w2.T,
         head_second_bias,
     )
+    grads = grads.reshape(peers, chunk, part)
     grads = lax.all_to_all(grads, everyone, 0, 0, tiled=True, axis_index_groups=wide)
+    grads = grads.reshape(blocks, chans, chunk, part)
     grads = pl.pallas_call(
         place_kernel,
         out_shape=pltpu.HBM((peers, chunk, part), BF16),
         in_specs=[vmem],
         out_specs=hbm,
-        scratch_shapes=[pltpu.SemaphoreType.DMA((2,))],
+        scratch_shapes=[pltpu.SemaphoreType.DMA((4,))],
         compiler_params=params,
         name="place",
     )(grads)

time: 75.1 us -> 75 us (level)
  no operation moved by 1% of the time
where the time goes in v7:
time: 75 us; the launch traced here: 74.7 us
  blocking collectives  65 us (87%)
  Pallas kernels  8.29 us (11%)
  between operations  1.37 us (2%)
    all_to_all x1, blocking collectives, local(): lax.all_to_all(both, everyone, 0, 0, tiled=True, axis_index_groups=wide)  33.2 us
    all_to_all x1, blocking collectives, local(): lax.all_to_all(grads, everyone, 0, 0, tiled=True, axis_index_groups=wide)  20.5 us
    all_to_all x1, blocking collectives, local(): pool = lax.all_to_all(pool, 'blk', 0, 0, tiled=True, axis_index_groups=near)  11.3 us
    pallas_call x1, Pallas kernels, local(): pl.pallas_call(lambda *refs: backward_kernel(blocks, chunk, *refs), out_s...  3.78 us
    pallas_call x1, Pallas kernels, local(): pl.pallas_call(lambda *refs: forward_kernel(blocks, chunk, *refs), out_sh...  2.7 us

profile of v7, /device:TPU:32, one launch (start us, length us, event | category | flops | bytes accessed | tf_op | source)
XLA Modules:
  0.0 74.7 jit_solution(10277874193428429601)
XLA Ops:
  1.3 0.0 copy-start
  1.3 0.0 copy-start.1
  1.3 0.0 copy-start.6
  1.3 1.1 %join.1 = (bf16[16,2,2,16,128]{4,3,2,1,0:T(8,128)(2,1)S(1)}, s32[8]{0:T(128)}) custom-call(s32[1]{0:T(128)S(6)} %copy.15.limit_ref, bf16[32,16,128]{2,1,0:T(8,128)(2,1)} %bitcast.19, bf16[32,16,128]{2,1,0:T(8,128)(2,1)} %bitcast.20), custom_call_target="tpu_custom_call" | custom-call | flops 40000000000 | bytes 524288 | tf_op jit(solution)/shard_map/join/pallas_call | solution.py:388
  2.4 33.2 %all_to_all.15 = bf16[32,2,16,128]{3,2,1,0:T(8,128)(2,1)S(1)} all-to-all(bf16[32,2,16,128]{3,2,1,0:T(8,128)(2,1)S(1)} %bitcast.13), channel_id=1, replica_groups={{321,320,353,352,385,384,417,416,449,448,481,480,1,0,33,32,65,64,97,96,..., dimensions={0} | all-to-all | bytes 524288 | tf_op jit(solution)/shard_map/all_to_all | solution.py:411
  35.6 0.0 copy-done
  35.6 0.0 copy-done.1
  35.6 0.0 copy-done.6
  35.6 0.0 copy-start.2
  35.6 0.0 copy-start.3
  35.7 0.0 copy-start.4
  35.7 0.0 copy-start.5
  35.7 2.7 %forward.1 = (bf16[4,256,512]{2,1,0:T(8,128)(2,1)}, bf16[256,256]{1,0:T(8,128)(2,1)S(1)}, bf16[16,24,256]{2,1,0:T(8,128)(2,1)S(1)}) custom-call(s32[8]{0:T(128)} %get-tuple-element.9.refs_0_, s32[4]{0:T(128)} %refs_1_.1, s32[4]{0:T(128)} %refs_2_.1, bf16[16,2,2,16,128]{4,3,2,1,0:T(8,128)(2,1)S(1)} %bitcast.12, bf16[4,2,256,512]{3,2,1,0:T(8,128)(2,1)S(1)} %copy-done, ...), custom_call_target="tpu_custom_call" | custom-call | flops 40000000000 | bytes 8388608 | tf_op jit(solution)/shard_map/forward/pallas_call | solution.py:414
  38.4 11.3 %all_to_all.16.refs_1_ = bf16[16,24,256]{2,1,0:T(8,128)(2,1)S(1)} all-to-all(bf16[16,24,256]{2,1,0:T(8,128)(2,1)S(1)} %get-tuple-element.11), channel_id=1, replica_groups={{320,352,384,416,448,480,0,32,64,96,128,160,192,224,256,288},{321,353,3..., dimensions={0} | all-to-all | bytes 393216 | tf_op jit(solution)/shard_map/all_to_all | solution.py:448
  49.7 0.0 copy-done.2
  49.7 0.0 copy-done.3
  49.7 0.0 copy-done.4
  49.7 0.0 copy-done.5
  49.7 3.8 %backward.1 = (f32[1,2]{1,0:T(1,128)}, bf16[16,2,16,128]{3,2,1,0:T(8,128)(2,1)S(1)}) custom-call(s32[8]{0:T(128)} %get-tuple-element.9.refs_0_, bf16[16,24,256]{2,1,0:T(8,128)(2,1)S(1)} %all_to_all.16.refs_1_, bf16[4,256,512]{2,1,0:T(8,128)(2,1)} %get-tuple-element.12.refs_2_, bf16[256,256]{1,0:T(8,128)(2,1)S(1)} %get-tuple-element.13.refs_3_, ...), custom_call_target="tpu_custom_call" | custom-call | tf_op jit(solution)/shard_map/backward/pallas_call | solution.py:452
  53.5 20.5 %all_to_all.17 = bf16[32,16,128]{2,1,0:T(8,128)(2,1)S(1)} all-to-all(bf16[32,16,128]{2,1,0:T(8,128)(2,1)S(1)} %bitcast.14), channel_id=1, replica_groups={{321,320,353,352,385,384,417,416,449,448,481,480,1,0,33,32,65,64,97,96,..., dimensions={0} | all-to-all | bytes 262144 | tf_op jit(solution)/shard_map/all_to_all | solution.py:484
  74.0 0.7 place.1
Async XLA Ops:
  1.3 34.3 %copy-start = (bf16[4,2,256,512]{3,2,1,0:T(8,128)(2,1)S(1)}, bf16[4,2,256,512]{3,2,1,0:T(8,128)(2,1)}, u32[]{:S(2)}) copy-start(bf16[4,2,256,512]{3,2,1,0:T(8,128)(2,1)} %refs_5_.3) | copy-start | bytes 6291460
  1.3 34.3 %copy-start.1 = (bf16[3,256,256]{2,1,0:T(8,128)(2,1)S(1)}, bf16[3,256,256]{2,1,0:T(8,128)(2,1)}, u32[]{:S(2)}) copy-start(bf16[3,256,256]{2,1,0:T(8,128)(2,1)} %refs_6_.3) | copy-start | bytes 1179652
  1.3 34.3 %copy-start.6 = (f32[4,512]{1,0:T(4,128)S(1)}, f32[4,512]{1,0:T(4,128)}, u32[]{:S(2)}) copy-start(f32[4,512]{1,0:T(4,128)} %refs_5_.2) | copy-start | bytes 24580
  35.6 14.1 %copy-start.2 = (f32[256,256]{1,0:T(8,128)S(1)}, f32[256,256]{1,0:T(8,128)}, u32[]{:S(2)}) copy-start(f32[256,256]{1,0:T(8,128)} %refs_7_.3) | copy-start | bytes 786436
  35.6 14.1 %copy-start.3 = (f32[256,12]{0,1:T(8,128)S(1)}, f32[256,12]{0,1:T(8,128)}, u32[]{:S(2)}) copy-start(f32[256,12]{0,1:T(8,128)} %param.21) | copy-start | bytes 36868
  35.7 14.1 %copy-start.4 = (f32[256]{0:T(256)S(1)}, f32[256]{0:T(256)}, u32[]{:S(2)}) copy-start(f32[256]{0:T(256)} %param.20) | copy-start | bytes 3076
  35.7 14.1 %copy-start.5 = (f32[12]{0:T(128)S(1)}, f32[12]{0:T(128)}, u32[]{:S(2)}) copy-start(f32[12]{0:T(128)} %param.22) | copy-start | bytes 148

commit v8 on v7

--- a/solution.py
+++ b/solution.py
@@ -46,8 +46,10 @@
 
 
 def row_keep(limit, base, blocks, chunk, width):
-    rows = lax.broadcasted_iota(jnp.int32, (blocks * chunk, width), 0)
-    position = (rows // chunk) * FIRST_DILATION + rows % chunk + base
+    shape = (blocks, chunk, width)
+    block = lax.broadcasted_iota(jnp.int32, shape, 0)
+    offset = lax.broadcasted_iota(jnp.int32, shape, 1)
+    position = (block * FIRST_DILATION + offset + base).reshape(blocks * chunk, width)
     return position < limit
 
 
@@ -297,15 +299,11 @@
         == 1.0
     )
     log_time = jnp.log((bins + 1.0) / 8.0)
-    window = lax.broadcasted_iota(jnp.int32, (2 * blocks, width), 0)
-    start = (
-        (window % blocks) * FIRST_DILATION
-        + shard_base
-        + (2 * chan_at + window // blocks) * WLEN
-    )
+    start = lax.broadcasted_iota(jnp.int32, (blocks, width), 0) * FIRST_DILATION
     limit_copy.wait()
-    limit = limit_ref[0]
-    count = jnp.clip(limit - start, 1, WLEN).astype(F32)
+    left = limit_ref[0] - shard_base - 2 * chan_at * WLEN
+    left = jnp.concatenate([left - start, left - WLEN - start], axis=0)
+    count = jnp.clip(left, 1, WLEN).astype(F32)
     pooled = sums / count
     pad_ref[...] = jnp.zeros_like(pad_ref)
     pad_ref[:outs, :] = head2_ref[...]

time: 75 us -> 75 us (level)
  no operation moved by 1% of the time
where the time goes in v8:
time: 75 us; the launch traced here: 74.7 us
  blocking collectives  65 us (87%)
  Pallas kernels  8.29 us (11%)
  between operations  1.37 us (2%)
    all_to_all x1, blocking collectives, local(): lax.all_to_all(both, everyone, 0, 0, tiled=True, axis_index_groups=wide)  33.2 us
    all_to_all x1, blocking collectives, local(): lax.all_to_all(grads, everyone, 0, 0, tiled=True, axis_index_groups=wide)  20.5 us
    all_to_all x1, blocking collectives, local(): pool = lax.all_to_all(pool, 'blk', 0, 0, tiled=True, axis_index_groups=near)  11.3 us
    pallas_call x1, Pallas kernels, local(): pl.pallas_call(lambda *refs: backward_kernel(blocks, chunk, *refs), out_s...  3.78 us
    pallas_call x1, Pallas kernels, local(): pl.pallas_call(lambda *refs: forward_kernel(blocks, chunk, *refs), out_sh...  2.7 us

profile of v8, /device:TPU:32, one launch (start us, length us, event | category | flops | bytes accessed | tf_op | source)
XLA Modules:
  0.0 74.7 jit_solution(13681535783097744970)
XLA Ops:
  1.3 0.0 copy-start
  1.3 0.0 copy-start.1
  1.3 0.0 copy-start.6
  1.3 1.1 %join.1 = (bf16[16,2,2,16,128]{4,3,2,1,0:T(8,128)(2,1)S(1)}, s32[8]{0:T(128)}) custom-call(s32[1]{0:T(128)S(6)} %copy.15.limit_ref, bf16[32,16,128]{2,1,0:T(8,128)(2,1)} %bitcast.19, bf16[32,16,128]{2,1,0:T(8,128)(2,1)} %bitcast.20), custom_call_target="tpu_custom_call" | custom-call | flops 40000000000 | bytes 524288 | tf_op jit(solution)/shard_map/join/pallas_call | solution.py:386
  2.4 33.2 %all_to_all.15 = bf16[32,2,16,128]{3,2,1,0:T(8,128)(2,1)S(1)} all-to-all(bf16[32,2,16,128]{3,2,1,0:T(8,128)(2,1)S(1)} %bitcast.13), channel_id=1, replica_groups={{321,320,353,352,385,384,417,416,449,448,481,480,1,0,33,32,65,64,97,96,..., dimensions={0} | all-to-all | bytes 524288 | tf_op jit(solution)/shard_map/all_to_all | solution.py:409
  35.6 0.0 copy-done
  35.6 0.0 copy-done.1
  35.6 0.0 copy-done.6
  35.6 0.0 copy-start.2
  35.6 0.0 copy-start.3
  35.7 0.0 copy-start.4
  35.7 0.0 copy-start.5
  35.7 2.7 %forward.1 = (bf16[4,256,512]{2,1,0:T(8,128)(2,1)}, bf16[256,256]{1,0:T(8,128)(2,1)S(1)}, bf16[16,24,256]{2,1,0:T(8,128)(2,1)S(1)}) custom-call(s32[8]{0:T(128)} %get-tuple-element.9.refs_0_, s32[4]{0:T(128)} %refs_1_.1, s32[4]{0:T(128)} %refs_2_.1, bf16[16,2,2,16,128]{4,3,2,1,0:T(8,128)(2,1)S(1)} %bitcast.12, bf16[4,2,256,512]{3,2,1,0:T(8,128)(2,1)S(1)} %copy-done, ...), custom_call_target="tpu_custom_call" | custom-call | flops 40000000000 | bytes 8388608 | tf_op jit(solution)/shard_map/forward/pallas_call | solution.py:412
  38.4 11.3 %all_to_all.16.refs_1_ = bf16[16,24,256]{2,1,0:T(8,128)(2,1)S(1)} all-to-all(bf16[16,24,256]{2,1,0:T(8,128)(2,1)S(1)} %get-tuple-element.11), channel_id=1, replica_groups={{320,352,384,416,448,480,0,32,64,96,128,160,192,224,256,288},{321,353,3..., dimensions={0} | all-to-all | bytes 393216 | tf_op jit(solution)/shard_map/all_to_all | solution.py:446
  49.7 0.0 copy-done.2
  49.7 0.0 copy-done.3
  49.7 0.0 copy-done.4
  49.7 0.0 copy-done.5
  49.7 3.8 %backward.1 = (f32[1,2]{1,0:T(1,128)}, bf16[16,2,16,128]{3,2,1,0:T(8,128)(2,1)S(1)}) custom-call(s32[8]{0:T(128)} %get-tuple-element.9.refs_0_, bf16[16,24,256]{2,1,0:T(8,128)(2,1)S(1)} %all_to_all.16.refs_1_, bf16[4,256,512]{2,1,0:T(8,128)(2,1)} %get-tuple-element.12.refs_2_, bf16[256,256]{1,0:T(8,128)(2,1)S(1)} %get-tuple-element.13.refs_3_, ...), custom_call_target="tpu_custom_call" | custom-call | tf_op jit(solution)/shard_map/backward/pallas_call | solution.py:450
  53.5 20.5 %all_to_all.17 = bf16[32,16,128]{2,1,0:T(8,128)(2,1)S(1)} all-to-all(bf16[32,16,128]{2,1,0:T(8,128)(2,1)S(1)} %bitcast.14), channel_id=1, replica_groups={{321,320,353,352,385,384,417,416,449,448,481,480,1,0,33,32,65,64,97,96,..., dimensions={0} | all-to-all | bytes 262144 | tf_op jit(solution)/shard_map/all_to_all | solution.py:482
  74.0 0.7 place.1
Async XLA Ops:
  1.3 34.3 %copy-start = (bf16[4,2,256,512]{3,2,1,0:T(8,128)(2,1)S(1)}, bf16[4,2,256,512]{3,2,1,0:T(8,128)(2,1)}, u32[]{:S(2)}) copy-start(bf16[4,2,256,512]{3,2,1,0:T(8,128)(2,1)} %refs_5_.3) | copy-start | bytes 6291460
  1.3 34.3 %copy-start.1 = (bf16[3,256,256]{2,1,0:T(8,128)(2,1)S(1)}, bf16[3,256,256]{2,1,0:T(8,128)(2,1)}, u32[]{:S(2)}) copy-start(bf16[3,256,256]{2,1,0:T(8,128)(2,1)} %refs_6_.3) | copy-start | bytes 1179652
  1.3 34.3 %copy-start.6 = (f32[4,512]{1,0:T(4,128)S(1)}, f32[4,512]{1,0:T(4,128)}, u32[]{:S(2)}) copy-start(f32[4,512]{1,0:T(4,128)} %refs_5_.2) | copy-start | bytes 24580
  35.6 14.1 %copy-start.2 = (f32[256,256]{1,0:T(8,128)S(1)}, f32[256,256]{1,0:T(8,128)}, u32[]{:S(2)}) copy-start(f32[256,256]{1,0:T(8,128)} %refs_7_.3) | copy-start | bytes 786436
  35.6 14.1 %copy-start.3 = (f32[256,12]{0,1:T(8,128)S(1)}, f32[256,12]{0,1:T(8,128)}, u32[]{:S(2)}) copy-start(f32[256,12]{0,1:T(8,128)} %param.21) | copy-start | bytes 36868
  35.7 14.1 %copy-start.4 = (f32[256]{0:T(256)S(1)}, f32[256]{0:T(256)}, u32[]{:S(2)}) copy-start(f32[256]{0:T(256)} %param.20) | copy-start | bytes 3076
  35.7 14.1 %copy-start.5 = (f32[12]{0:T(128)S(1)}, f32[12]{0:T(128)}, u32[]{:S(2)}) copy-start(f32[12]{0:T(128)} %param.22) | copy-start | bytes 148
